TPU v7x, 32 devices: a whole 2x2x4 slice. The times are simulated.
32 devices in a mesh: gx: 4 (over y, x), gy: 4 (over z), gz: 2 (over core).
Axes of the slice: x: 2, y: 2, z: 4, core: 2. Of those that a mesh axis runs over, the one named last changes fastest.
Arguments:
- populations: float32 [19, 32, 32, 512], P(None, 'gx', 'gz', 'gy'), may hold values from 0.005 to 0.6, as said below
- link_cell: int32 [4, 2, 4, 1024], P('gx', 'gz', 'gy'), may hold values from 0 to 16383, as said below
- link_dir: int32 [4, 2, 4, 1024], P('gx', 'gz', 'gy'), may hold values from 0 to 18, as said below
- link_slot: int32 [4, 2, 4, 1024], P('gx', 'gz', 'gy'), may hold values from 0 to 127, as said below
- link_arm: float32 [3, 4, 2, 4, 1024], P(None, 'gx', 'gz', 'gy'), may hold values from -6 to 6
- brick_bodies: int32 [4, 2, 4, 128], P('gx', 'gz', 'gy'), may hold values from 0 to 2047, as said below
- body_pos: float32 [3, 2048], P(None, ('gx', 'gy')), may hold values from -1 to 1
- body_quat: float32 [4, 2048], P(None, ('gx', 'gy')), may hold values from -1 to 1, as said below
- body_vel: float32 [3, 2048], P(None, ('gx', 'gy')), may hold values from -0.4 to 0.4
- body_spin: float32 [3, 2048], P(None, ('gx', 'gy')), may hold values from -0.4 to 0.4
- inv_mass: float32 [2048], P(('gx', 'gy')), may hold values from 0.5 to 4
- inv_inertia: float32 [3, 2048], P(None, ('gx', 'gy')), may hold values from 0.2 to 2
Outputs:
- next_populations: float32 [19, 32, 32, 512], P(None, 'gx', 'gz', 'gy')
- body_next: float32 [13, 2048], P(None, ('gx', 'gy'))
Inputs may be any that keep to these rules, and one draw needn't show every extreme that they name: `populations`: every entry is positive, and the density (sum over the 19 directions) at every cell lies between 0.5 and 1.6. `link_cell`: within a brick all entries name different cells. `link_dir`: within a brick the used entries (direction 1 to 18) come first, unused ones have direction 0; some brick uses all 1024 entries in every draw. `link_slot`: unused entries hold 0. `brick_bodies`: each brick lists 128 different bodies; owner k holds bodies k*128 to (k+1)*128 - 1; a brick lists at most 16 bodies of one owner, and exactly 16 of some owner in every brick. `body_quat`: unit quaternions.
All inputs are finite; a program needn't handle non-finite values.
Results may differ from a plain program's by a relative error of at most 0.00013.
Values sent between devices are 32-bit elements; how exact they have to be, the bound alone decides.
A program may use at most 64 MiB of HBM per device.

v0:
```python
import jax
import jax.numpy as jnp
import numpy as np
from jax import lax
from jax.sharding import PartitionSpec as P

lattice_vel = np.array(
    [
        [0, 0, 0],
        [1, 0, 0],
        [-1, 0, 0],
        [0, 1, 0],
        [0, -1, 0],
        [0, 0, 1],
        [0, 0, -1],
        [1, 1, 0],
        [-1, -1, 0],
        [1, -1, 0],
        [-1, 1, 0],
        [1, 0, 1],
        [-1, 0, -1],
        [1, 0, -1],
        [-1, 0, 1],
        [0, 1, 1],
        [0, -1, -1],
        [0, 1, -1],
        [0, -1, 1],
    ]
)
lattice_wt = np.array([1.0 / 3.0] + [1.0 / 18.0] * 6 + [1.0 / 36.0] * 12)
opposite_dir = np.array([0, 2, 1, 4, 3, 6, 5, 8, 7, 10, 9, 12, 11, 14, 13, 16, 15, 18, 17])
omega_relax = 1.25
grav_accel = 0.02


def padded_2(block, sides, width):
    for axis, dim in sides:
        count = lax.axis_size(axis)
        forward = [(i, i + 1) for i in range(count - 1)]
        forward.append((count - 1, 0))
        backward = [(target, source) for source, target in forward]
        low = lax.ppermute(
            lax.slice_in_dim(block, block.shape[dim] - width, None, axis=dim), axis, forward
        )
        high = lax.ppermute(lax.slice_in_dim(block, 0, width, axis=dim), axis, backward)
        block = jnp.concatenate([low, block, high], axis=dim)
    return block


def collide(populations):
    density = populations[0]
    for direction in range(1, 19):
        density = density + populations[direction]
    flows = []
    for comp_index in range(3):
        total = jnp.zeros_like(density)
        for direction in range(19):
            if lattice_vel[direction, comp_index] == 1:
                total = total + populations[direction]
            elif lattice_vel[direction, comp_index] == -1:
                total = total - populations[direction]
        flows.append(total / density)
    speed_sq = flows[0] * flows[0] + flows[1] * flows[1] + flows[2] * flows[2]
    relaxed = []
    for direction in range(19):
        proj = (
            float(lattice_vel[direction, 0]) * flows[0]
            + float(lattice_vel[direction, 1]) * flows[1]
            + float(lattice_vel[direction, 2]) * flows[2]
        )
        equil = (
            float(lattice_wt[direction])
            * density
            * (1.0 + 3.0 * proj + 4.5 * proj * proj - 1.5 * speed_sq)
        )
        relaxed.append(populations[direction] - omega_relax * (populations[direction] - equil))
    return jnp.stack(relaxed)


def link_terms(post_out, link_dirs, arm, motion_at):
    iota_dir = jnp.arange(19, dtype=jnp.int32)
    onehot = (link_dirs[None, :] == iota_dir[:, None]).astype(jnp.float32)
    table = jnp.asarray(np.concatenate([lattice_vel.T, lattice_wt[None, :]], 0), jnp.float32)
    coeffs = jnp.dot(table, onehot, precision=lax.Precision.HIGHEST)
    vel_x, vel_y, vel_z = (coeffs[0], coeffs[1], coeffs[2])
    weight = coeffs[3]
    opp_table = jnp.asarray(opposite_dir, jnp.int32)
    opp_dir = jnp.sum(
        opp_table[:, None] * (link_dirs[None, :] == iota_dir[:, None]).astype(jnp.int32), 0
    )
    wall_x = motion_at[0] + motion_at[4] * arm[2] - motion_at[5] * arm[1]
    wall_y = motion_at[1] + motion_at[5] * arm[0] - motion_at[3] * arm[2]
    wall_z = motion_at[2] + motion_at[3] * arm[1] - motion_at[4] * arm[0]
    proj = vel_x * wall_x + vel_y * wall_y + vel_z * wall_z
    bounce = post_out - 6.0 * weight * proj
    live = (link_dirs > 0).astype(jnp.float32)
    exchanged = (post_out + bounce) * live
    force_x, force_y, force_z = (vel_x * exchanged, vel_y * exchanged, vel_z * exchanged)
    torque_x = arm[1] * force_z - arm[2] * force_y
    torque_y = arm[2] * force_x - arm[0] * force_z
    torque_z = arm[0] * force_y - arm[1] * force_x
    loads = jnp.stack([force_x, force_y, force_z, torque_x, torque_y, torque_z])
    return (bounce, live, opp_dir, loads)


def integrate(body_pos, body_quat, body_vel, body_spin, inv_mass, inv_inertia, load):
    gravity = jnp.asarray(np.array([0.0, 0.0, -grav_accel]), jnp.float32)[:, None]
    velocity = body_vel + inv_mass[None, :] * load[0:3] + gravity
    quat_w, quat_x, quat_y, quat_z = (body_quat[0], body_quat[1], body_quat[2], body_quat[3])
    rotation = [
        [
            1.0 - 2.0 * (quat_y * quat_y + quat_z * quat_z),
            2.0 * (quat_x * quat_y - quat_w * quat_z),
            2.0 * (quat_x * quat_z + quat_w * quat_y),
        ],
        [
            2.0 * (quat_x * quat_y + quat_w * quat_z),
            1.0 - 2.0 * (quat_x * quat_x + quat_z * quat_z),
            2.0 * (quat_y * quat_z - quat_w * quat_x),
        ],
        [
            2.0 * (quat_x * quat_z - quat_w * quat_y),
            2.0 * (quat_y * quat_z + quat_w * quat_x),
            1.0 - 2.0 * (quat_x * quat_x + quat_y * quat_y),
        ],
    ]
    torque = load[3:6]
    frame_torque = [
        rotation[0][col] * torque[0] + rotation[1][col] * torque[1] + rotation[2][col] * torque[2]
        for col in range(3)
    ]
    frame_accel = [inv_inertia[col] * frame_torque[col] for col in range(3)]
    accel = [
        rotation[row][0] * frame_accel[0]
        + rotation[row][1] * frame_accel[1]
        + rotation[row][2] * frame_accel[2]
        for row in range(3)
    ]
    spin = body_spin + jnp.stack(accel)
    position = body_pos + velocity
    spin_x, spin_y, spin_z = (spin[0], spin[1], spin[2])
    delta_w = -(spin_x * quat_x + spin_y * quat_y + spin_z * quat_z)
    delta_x = spin_x * quat_w + spin_y * quat_z - spin_z * quat_y
    delta_y = spin_y * quat_w + spin_z * quat_x - spin_x * quat_z
    delta_z = spin_z * quat_w + spin_x * quat_y - spin_y * quat_x
    scale = lax.rsqrt(1.0 + 0.25 * (spin_x * spin_x + spin_y * spin_y + spin_z * spin_z))
    quat = (
        jnp.stack(
            [
                quat_w + 0.5 * delta_w,
                quat_x + 0.5 * delta_x,
                quat_y + 0.5 * delta_y,
                quat_z + 0.5 * delta_z,
            ]
        )
        * scale[None, :]
    )
    return jnp.concatenate([position, quat, velocity, spin], 0)


def shards(
    populations,
    link_cell,
    link_dir,
    link_slot,
    link_arm,
    brick_bodies,
    body_pos,
    body_quat,
    body_vel,
    body_spin,
    inv_mass,
    inv_inertia,
):
    relaxed = collide(populations)
    span_x, span_z, span_y = (relaxed.shape[1], relaxed.shape[2], relaxed.shape[3])
    padded = padded_2(relaxed, (("gx", 1), ("gz", 2), ("gy", 3)), 1)
    pieces = []
    for direction in range(19):
        off_x = 1 - int(lattice_vel[direction, 0])
        off_z = 1 - int(lattice_vel[direction, 2])
        off_y = 1 - int(lattice_vel[direction, 1])
        pieces.append(
            padded[
                direction, off_x : off_x + span_x, off_z : off_z + span_z, off_y : off_y + span_y
            ]
        )
    read = jnp.stack(pieces)
    cell_idx = link_cell.reshape(-1)
    link_dirs = link_dir.reshape(-1)
    slot_of = link_slot.reshape(-1)
    arm = link_arm.reshape(3, -1)
    slot_bodies = brick_bodies.reshape(-1)
    slot_count = slot_bodies.shape[0]
    body_own = body_vel.shape[1]
    own_motion = jnp.concatenate([body_vel, body_spin], 0)
    slot_onehot = (slot_of[None, :] == jnp.arange(slot_count, dtype=jnp.int32)[:, None]).astype(
        jnp.float32
    )
    owner_count = lax.axis_size(("gx", "gy"))
    bucket_cap = max(2, 2 * slot_count // owner_count)
    owner_of = slot_bodies // body_own
    local_id = slot_bodies - owner_of * body_own
    slot_iota = jnp.arange(slot_count, dtype=jnp.int32)
    earlier = (owner_of[None, :] == owner_of[:, None]) & (slot_iota[None, :] < slot_iota[:, None])
    bucket_rank = jnp.sum(earlier.astype(jnp.int32), 1)
    bucket_pos = owner_of * bucket_cap + bucket_rank
    wanted = jnp.full((owner_count * bucket_cap,), -1, jnp.int32).at[bucket_pos].set(local_id)
    asked = lax.all_to_all(
        wanted.reshape(owner_count, bucket_cap),
        ("gx", "gy"),
        split_axis=0,
        concat_axis=0,
        tiled=True,
    )
    asked_flat = asked.reshape(-1)
    valid = asked_flat >= 0
    safe_id = jnp.where(valid, asked_flat, 0)
    answer = own_motion[:, safe_id] * valid.astype(jnp.float32)[None, :]
    answer = answer.reshape(6, asked.shape[0], bucket_cap)
    returned = lax.all_to_all(answer, ("gx", "gy"), split_axis=1, concat_axis=1, tiled=True)
    slot_motion = returned.reshape(6, -1)[:, bucket_pos]
    motion_at = jnp.dot(slot_motion, slot_onehot, precision=lax.Precision.HIGHEST)
    flat_relaxed = relaxed.reshape(19, -1)
    post_out = flat_relaxed[link_dirs, cell_idx]
    bounce, live, opp_dir, loads = link_terms(post_out, link_dirs, arm, motion_at)
    flat_stream = read.reshape(19, -1)
    current = flat_stream[opp_dir, cell_idx]
    next_populations = (
        flat_stream.at[opp_dir, cell_idx].add(live * (bounce - current)).reshape(read.shape)
    )
    partial_value = jnp.dot(loads, slot_onehot.T, precision=lax.Precision.HIGHEST)
    outgoing = (
        jnp.zeros((6, owner_count * bucket_cap), jnp.float32).at[:, bucket_pos].set(partial_value)
    )
    incoming = lax.all_to_all(
        outgoing.reshape(6, owner_count, bucket_cap),
        ("gx", "gy"),
        split_axis=1,
        concat_axis=1,
        tiled=True,
    )
    owner_onehot = (
        (safe_id[:, None] == jnp.arange(body_own, dtype=jnp.int32)[None, :]) & valid[:, None]
    ).astype(jnp.float32)
    plane = jnp.dot(incoming.reshape(6, -1), owner_onehot, precision=lax.Precision.HIGHEST)
    load = lax.psum(plane, "gz")
    return (
        next_populations,
        integrate(body_pos, body_quat, body_vel, body_spin, inv_mass, inv_inertia, load),
    )


def solution(mesh):
    return jax.shard_map(
        shards,
        mesh=mesh,
        in_specs=(
            P(None, "gx", "gz", "gy"),
            P("gx", "gz", "gy", None),
            P("gx", "gz", "gy", None),
            P("gx", "gz", "gy", None),
            P(None, "gx", "gz", "gy", None),
            P("gx", "gz", "gy", None),
            P(None, ("gx", "gy")),
            P(None, ("gx", "gy")),
            P(None, ("gx", "gy")),
            P(None, ("gx", "gy")),
            P(("gx", "gy")),
            P(None, ("gx", "gy")),
        ),
        out_specs=(P(None, "gx", "gz", "gy"), P(None, ("gx", "gy"))),
        check_vma=False,
    )
```

profile of v0, /device:TPU:0, one launch (start us, length us, event | category | flops | bytes accessed | tf_op | source)
XLA Modules:
  0.0 127.4 jit_solution(8612535991600105244)
XLA Ops:
  0.6 0.8 bitcast_subtract_fusion
  2.3 1.0 scatter_custom_fusion
  3.9 8.3 %all-to-all-start = ((s32[16,1,16]{2,1,0:T(1,128)}), s32[16,1,16]{2,1,0:T(1,128)S(1)}, u32[]{:S(2)}, u32[]{:S(2)}) async-start(s32[16,1,16]{2,1,0:T(1,128)} %all_to_all.12), calls=%async_computation | async-start | bytes 16384 | tf_op jit(solution)/shard_map/all_to_all | solution.py:209
  12.3 1.5 %constant_dynamic-update-slice_fusion.18 = (f32[19,8,16,128]{3,2,1,0:T(8,128)S(1)}, f32[1,8,16,128]{3,2,1,0:T(8,128)S(1)}, f32[1,8,16,128]{3,2,1,0:T(8,128)S(1)}...) fusion(f32[19,8,16,128]{3,2,1,0:T(8,128)} %param.15), kind=kLoop, calls=%fused_computation.221 | loop fusion | flops 1146879 | bytes 1703936
  24.1 1.9 %collective-permute-start = (f32[19,1,16,128]{3,2,1,0:T(8,128)}, f32[19,1,16,128]{3,2,1,0:T(8,128)S(1)}, u32[]{:S(2)}, u32[]{:S(2)}) collective-permute-start(f32[19,1,16,128]{3,2,1,0:T(8,128)} %get-tuple-element.82), channel_id=1, source_target_pairs={{0,8},{8,16},{16,24},{24,0},{1,9},{9,17},{17,25},{25,1},{2,10},{10... | collective-permute-start | bytes 466952 | tf_op jit(solution)/shard_map/ppermute | solution.py:42
  26.0 1.0 collective-permute-start.1
  27.8 0.8 fusion.7
  30.0 4.3 %stack.162 = f32[19,16384]{1,0:T(8,128)S(1)} concatenate(f32[1,16384]{1,0:T(1,128)S(1)} %bitcast.181, f32[1,16384]{1,0:T(1,128)S(1)} %bitcast.202, f32[1,16384]{1,0:T(1,128)S(1)} %bitcast.203, f32[1,16384]{1,0:T(1,128)S(1)} %bitcast.204, f32[1,16384]{1,0:T(1,128)S(1)} %bitcast.205, f32[1,16384]{1,0:T(1,128)} %bitcast.206, f32[1,16384]{1,0:T(1,128)} %bitcast.207, ...), dimensions={0} | concatenate | bytes 2490368 | tf_op jit(solution)/shard_map/stack | solution.py:77
  34.4 8.6 %gather_fusion = f32[1024]{0:T(1024)S(1)} fusion(f32[19,16384]{1,0:T(8,128)S(1)} %stack.162, s32[1024]{0:T(1024)S(1)} %bitcast.179), kind=kCustom, calls=%fused_computation | custom fusion | bytes 16384 | tf_op jit(solution)/shard_map/gather | solution.py:225
  45.9 6.0 %all-to-all-start.1 = ((f32[6,16,16]{2,0,1:T(8,128)}), f32[6,16,16]{2,0,1:T(8,128)S(1)}, u32[]{:S(2)}, u32[]{:S(2)}) async-start(f32[6,16,16]{2,0,1:T(8,128)} %broadcast_multiply_fusion), calls=%async_computation.1 | async-start | bytes 131072 | tf_op jit(solution)/shard_map/all_to_all | solution.py:221
  52.0 7.3 %all-to-all-done.1 = f32[6,16,16]{2,0,1:T(8,128)S(1)} async-done(((f32[6,16,16]{2,0,1:T(8,128)}), f32[6,16,16]{2,0,1:T(8,128)S(1)}, u32[]{:S(2)}, u32[]{:S(2)}) %all-to-all-start.1) | async-done | bytes 6176 | tf_op jit(solution)/shard_map/all_to_all | solution.py:221
  59.6 0.8 gather_fusion.2
  62.3 1.0 scatter_custom_fusion.1
  63.3 0.8 copy.123
  64.1 3.5 %all-to-all-start.2 = ((f32[6,16,16]{2,0,1:T(8,128)}), f32[6,16,16]{2,0,1:T(8,128)S(1)}, u32[]{:S(2)}, u32[]{:S(2)}) async-start(f32[6,16,16]{2,0,1:T(8,128)} %copy.123), calls=%async_computation.2 | async-start | bytes 131072 | tf_op jit(solution)/shard_map/all_to_all | solution.py:236
  67.6 7.4 %all-to-all-done.2 = f32[6,16,16]{2,0,1:T(8,128)S(1)} async-done(((f32[6,16,16]{2,0,1:T(8,128)}), f32[6,16,16]{2,0,1:T(8,128)S(1)}, u32[]{:S(2)}, u32[]{:S(2)}) %all-to-all-start.2) | async-done | bytes 6176 | tf_op jit(solution)/shard_map/all_to_all | solution.py:236
  75.4 2.5 %psum.7 = f32[6,128]{1,0:T(8,128)S(1)} all-reduce(f32[6,128]{1,0:T(8,128)S(1)} %fusion.5), channel_id=1, replica_groups=mesh['gx'=4,'gy'=4,'gz'=2] {'gz'}, use_global_device_ids=true, to_apply=%region_5.6 | all-reduce | flops 768 | bytes 6144 | tf_op jit(solution)/shard_map/psum | solution.py:247
  80.4 2.9 %fusion.168 = (f32[19,10,18,1]{3,2,1,0:T(8,128)}, f32[19,10,18,1]{3,2,1,0:T(8,128)}) fusion(f32[19,10,18,128]{3,2,1,0:T(8,128)S(1)} %pad_maximum_fusion), kind=kLoop, calls=%fused_computation.318 | loop fusion | bytes 54720 | tf_op jit(solution)/shard_map/slice | solution.py:45
  83.3 3.1 %copy.113 = f32[19,10,18,1]{2,0,3,1:T(8,128)S(1)} copy(f32[19,10,18,1]{3,2,1,0:T(8,128)} %get-tuple-element.70) | data formatting | bytes 27360 | tf_op jit(solution)/shard_map/slice | solution.py:43
  86.4 0.9 collective-permute-start.4
  87.4 3.1 %copy.115 = f32[19,10,18,1]{2,0,3,1:T(8,128)S(1)} copy(f32[19,10,18,1]{3,2,1,0:T(8,128)} %get-tuple-element.69) | data formatting | bytes 27360 | tf_op jit(solution)/shard_map/slice | solution.py:45
  90.5 3.1 %collective-permute-start.5 = (f32[19,10,18,1]{2,0,3,1:T(8,128)S(1)}, f32[19,10,18,1]{2,0,3,1:T(8,128)S(1)}, u32[]{:S(2)}, u32[]{:S(2)}) collective-permute-start(f32[19,10,18,1]{2,0,3,1:T(8,128)S(1)} %copy.115), channel_id=1, source_target_pairs={{2,0},{4,2},{6,4},{0,6},{3,1},{5,3},{7,5},{1,7},{10,8},{12,10},{14... | collective-permute-start | bytes 41048 | tf_op jit(solution)/shard_map/ppermute | solution.py:45
  95.0 1.4 %collective-permute-done.5 = f32[19,10,18,1]{2,0,3,1:T(8,128)S(1)} collective-permute-done((f32[19,10,18,1]{2,0,3,1:T(8,128)S(1)}, f32[19,10,18,1]{2,0,3,1:T(8,128)S(1)}, u32[]{:S(2)}, u32[]{:S(2)}) %collective-permute-start.5) | collective-permute-done | bytes 13712 | tf_op jit(solution)/shard_map/ppermute | solution.py:45
  96.5 2.6 %copy.116 = f32[19,10,18,1]{3,2,1,0:T(8,128)} copy(f32[19,10,18,1]{2,0,3,1:T(8,128)S(1)} %collective-permute-done.5) | data formatting | bytes 27360 | tf_op jit(solution)/shard_map/ppermute | solution.py:45
  99.1 1.3 %pad_maximum_fusion.4 = (f32[1,8,16,128]{3,2,1,0:T(8,128)S(1)}, f32[1,8,16,128]{3,2,1,0:T(8,128)S(1)}, f32[1,8,16,128]{3,2,1,0:T(8,128)S(1)}) fusion(f32[19,10,18,1]{3,2,1,0:T(8,128)} %copy.116, f32[19,10,1,128]{3,2,1,0:T(1,128)S(1)} %copy.112, f32[19,10,1,128]{3,2,1,0:T(1,128)S(1)} %copy.111, f32[19,1,16,128]{3,2,1,0:T(8,128)S(1)} %collective-permute-done.1, ...), kind=kLoop, calls=%fused_computation.155 | loop fusion | flops 245760 | bytes 1961328 | tf_op jit(solution)/shard_map/concatenate | solution.py:46
  101.1 2.6 %copy.114 = f32[19,10,18,1]{3,2,1,0:T(8,128)} copy(f32[19,10,18,1]{2,0,3,1:T(8,128)S(1)} %collective-permute-done.4) | data formatting | bytes 27360 | tf_op jit(solution)/shard_map/ppermute | solution.py:42
  103.7 1.9 %pad_maximum_fusion.9 = (f32[1,8,16,128]{3,2,1,0:T(8,128)}, f32[1,8,16,128]{3,2,1,0:T(8,128)}, f32[1,8,16,128]{3,2,1,0:T(8,128)}) fusion(f32[19,10,18,1]{3,2,1,0:T(8,128)} %copy.114, f32[19,10,1,128]{3,2,1,0:T(1,128)S(1)} %copy.112, f32[19,10,1,128]{3,2,1,0:T(1,128)S(1)} %copy.111, f32[19,1,16,128]{3,2,1,0:T(8,128)S(1)} %collective-permute-done.1, ...), kind=kLoop, calls=%fused_computation.160 | loop fusion | flops 245760 | bytes 1961328 | tf_op jit(solution)/shard_map/concatenate | solution.py:46
  105.6 0.8 pad_maximum_fusion.27
  106.4 4.3 %stack.143 = f32[19,16384]{1,0:T(8,128)S(1)} concatenate(f32[1,16384]{1,0:T(1,128)S(1)} %bitcast.182, f32[1,16384]{1,0:T(1,128)} %bitcast.197, f32[1,16384]{1,0:T(1,128)} %bitcast.198, f32[1,16384]{1,0:T(1,128)} %bitcast.193, f32[1,16384]{1,0:T(1,128)S(1)} %bitcast.188, f32[1,16384]{1,0:T(1,128)} %bitcast.196, f32[1,16384]{1,0:T(1,128)} %bitcast.201, f32[1,16384]{1,0:T(1,128)} %bitcast.192, ...), dimensions={0} | concatenate | bytes 2490368 | tf_op jit(solution)/shard_map/stack | solution.py:188
  111.1 8.6 %gather_fusion.3 = f32[1024]{0:T(1024)S(1)} fusion(f32[19,16384]{1,0:T(8,128)S(1)} %stack.143, s32[1024]{0:T(1024)S(1)} %bitcast.178), kind=kCustom, calls=%fused_computation.3 | custom fusion | bytes 16384 | tf_op jit(solution)/shard_map/gather | solution.py:228
  119.8 6.5 %scatter_fusion = f32[311296]{0:T(1024)S(1)} fusion(f32[311296]{0:T(1024)S(1)} %reshape.394, s32[1024]{0:T(1024)S(1)} %copy-done.10, f32[1024]{0:T(1024)S(1)} %subtract_select_fusion), kind=kCustom, calls=%fused_computation.6 | custom fusion | flops 1024 | bytes 16384
  126.3 1.0 copy-done
  (151 shorter events, 24.2 us)
Async XLA Ops:
  0.6 13.1 %copy-start.3 = (f32[19,8,16,128]{3,2,1,0:T(8,128)S(1)}, f32[19,8,16,128]{3,2,1,0:T(8,128)}, u32[]{:S(2)}) copy-start(f32[19,8,16,128]{3,2,1,0:T(8,128)} %param.15) | copy-start | bytes 3735556
  2.3 24.7 %copy-start.30 = (s32[128]{0:T(128)}, s32[128]{0:T(128)S(1)}, u32[]{:S(2)}) copy-start(s32[128]{0:T(128)S(1)} %fusion.145) | copy-start | bytes 1540
  3.9 39.2 %all-to-all-start = ((s32[16,1,16]{2,1,0:T(1,128)}), s32[16,1,16]{2,1,0:T(1,128)S(1)}, u32[]{:S(2)}, u32[]{:S(2)}) async-start(s32[16,1,16]{2,1,0:T(1,128)} %all_to_all.12), calls=%async_computation | async-start | bytes 16384 | tf_op jit(solution)/shard_map/all_to_all | solution.py:209
  24.1 54.0 %collective-permute-start = (f32[19,1,16,128]{3,2,1,0:T(8,128)}, f32[19,1,16,128]{3,2,1,0:T(8,128)S(1)}, u32[]{:S(2)}, u32[]{:S(2)}) collective-permute-start(f32[19,1,16,128]{3,2,1,0:T(8,128)} %get-tuple-element.82), channel_id=1, source_target_pairs={{0,8},{8,16},{16,24},{24,0},{1,9},{9,17},{17,25},{25,1},{2,10},{10... | collective-permute-start | bytes 466952 | tf_op jit(solution)/shard_map/ppermute | solution.py:42
  26.0 52.1 %collective-permute-start.1 = (f32[19,1,16,128]{3,2,1,0:T(8,128)}, f32[19,1,16,128]{3,2,1,0:T(8,128)S(1)}, u32[]{:S(2)}, u32[]{:S(2)}) collective-permute-start(f32[19,1,16,128]{3,2,1,0:T(8,128)} %get-tuple-element.81), channel_id=1, source_target_pairs={{8,0},{16,8},{24,16},{0,24},{9,1},{17,9},{25,17},{1,25},{10,2},{18... | collective-permute-start | bytes 466952 | tf_op jit(solution)/shard_map/ppermute | solution.py:45
  34.4 26.0 %copy-start.34 = (s32[1,1,1,1024]{3,2,1,0:T(1,128)S(1)}, s32[1,1,1,1024]{3,2,1,0:T(1,128)}, u32[]{:S(2)}) copy-start(s32[1,1,1,1024]{3,2,1,0:T(1,128)} %param.18) | copy-start | bytes 12292
  34.4 26.2 %copy-start.6 = (f32[4,1024]{1,0:T(4,128)S(1)}, f32[4,1024]{1,0:T(4,128)}, u32[]{:S(2)}) copy-start(f32[4,1024]{1,0:T(4,128)} %fusion.7) | copy-start | bytes 49156
  43.0 35.3 %copy-start.7 = (f32[1024]{0:T(1024)}, f32[1024]{0:T(1024)S(1)}, u32[]{:S(2)}) copy-start(f32[1024]{0:T(1024)S(1)} %gather_fusion) | copy-start | bytes 12292
  43.0 34.9 %copy-start.9 = (f32[4,128]{1,0:T(4,128)S(1)}, f32[4,128]{1,0:T(4,128)}, u32[]{:S(2)}) copy-start(f32[4,128]{1,0:T(4,128)} %param.22) | copy-start | bytes 6148
  43.0 34.9 %copy-start.27 = (f32[3,128]{1,0:T(4,128)S(1)}, f32[3,128]{1,0:T(4,128)}, u32[]{:S(2)}) copy-start(f32[3,128]{1,0:T(4,128)} %param.26) | copy-start | bytes 4612
  43.0 34.9 %copy-start.22 = (f32[3,128]{1,0:T(4,128)S(1)}, f32[3,128]{1,0:T(4,128)}, u32[]{:S(2)}) copy-start(f32[3,128]{1,0:T(4,128)} %param.24) | copy-start | bytes 4612
  43.0 34.9 %copy-start.24 = (f32[3,128]{1,0:T(4,128)S(1)}, f32[3,128]{1,0:T(4,128)}, u32[]{:S(2)}) copy-start(f32[3,128]{1,0:T(4,128)} %param.23) | copy-start | bytes 4612
  43.0 34.9 %copy-start.26 = (f32[3,128]{1,0:T(4,128)S(1)}, f32[3,128]{1,0:T(4,128)}, u32[]{:S(2)}) copy-start(f32[3,128]{1,0:T(4,128)} %param.21) | copy-start | bytes 4612
  43.1 34.9 %copy-start.28 = (f32[128]{0:T(128)S(1)}, f32[128]{0:T(128)}, u32[]{:S(2)}) copy-start(f32[128]{0:T(128)} %param.25) | copy-start | bytes 1540
  43.1 34.9 %copy-start.29 = (f32[3]{0:T(128)S(1)}, f32[3]{0:T(128)}, u32[]{:S(2)}) copy-start(f32[3]{0:T(128)} %constant.73.clone) | copy-start | bytes 40
  45.9 13.5 %all-to-all-start.1 = ((f32[6,16,16]{2,0,1:T(8,128)}), f32[6,16,16]{2,0,1:T(8,128)S(1)}, u32[]{:S(2)}, u32[]{:S(2)}) async-start(f32[6,16,16]{2,0,1:T(8,128)} %broadcast_multiply_fusion), calls=%async_computation.1 | async-start | bytes 131072 | tf_op jit(solution)/shard_map/all_to_all | solution.py:221
  64.1 10.9 %all-to-all-start.2 = ((f32[6,16,16]{2,0,1:T(8,128)}), f32[6,16,16]{2,0,1:T(8,128)S(1)}, u32[]{:S(2)}, u32[]{:S(2)}) async-start(f32[6,16,16]{2,0,1:T(8,128)} %copy.123), calls=%async_computation.2 | async-start | bytes 131072 | tf_op jit(solution)/shard_map/all_to_all | solution.py:236
  78.3 1.4 %collective-permute-start.2 = (f32[19,10,1,128]{3,0,2,1:T(8,128)S(1)}, f32[19,10,1,128]{3,0,2,1:T(8,128)S(1)}, u32[]{:S(2)}, u32[]{:S(2)}) collective-permute-start(f32[19,10,1,128]{3,0,2,1:T(8,128)S(1)} %copy.109), channel_id=1, source_target_pairs={{0,1},{1,0},{2,3},{3,2},{4,5},{5,4},{6,7},{7,6},{8,9},{9,8},{10,11... | collective-permute-start | bytes 291848 | tf_op jit(solution)/shard_map/ppermute | solution.py:42
  78.5 1.4 %collective-permute-start.3 = (f32[19,10,1,128]{3,0,2,1:T(8,128)S(1)}, f32[19,10,1,128]{3,0,2,1:T(8,128)S(1)}, u32[]{:S(2)}, u32[]{:S(2)}) collective-permute-start(f32[19,10,1,128]{3,0,2,1:T(8,128)S(1)} %copy.110), channel_id=1, source_target_pairs={{1,0},{0,1},{3,2},{2,3},{5,4},{4,5},{7,6},{6,7},{9,8},{8,9},{11,10... | collective-permute-start | bytes 291848 | tf_op jit(solution)/shard_map/ppermute | solution.py:45
  86.4 14.6 %collective-permute-start.4 = (f32[19,10,18,1]{2,0,3,1:T(8,128)S(1)}, f32[19,10,18,1]{2,0,3,1:T(8,128)S(1)}, u32[]{:S(2)}, u32[]{:S(2)}) collective-permute-start(f32[19,10,18,1]{2,0,3,1:T(8,128)S(1)} %copy.113), channel_id=1, source_target_pairs={{0,2},{2,4},{4,6},{6,0},{1,3},{3,5},{5,7},{7,1},{8,10},{10,12},{12... | collective-permute-start | bytes 41048 | tf_op jit(solution)/shard_map/ppermute | solution.py:42
  90.5 6.0 %collective-permute-start.5 = (f32[19,10,18,1]{2,0,3,1:T(8,128)S(1)}, f32[19,10,18,1]{2,0,3,1:T(8,128)S(1)}, u32[]{:S(2)}, u32[]{:S(2)}) collective-permute-start(f32[19,10,18,1]{2,0,3,1:T(8,128)S(1)} %copy.115), channel_id=1, source_target_pairs={{2,0},{4,2},{6,4},{0,6},{3,1},{5,3},{7,5},{1,7},{10,8},{12,10},{14... | collective-permute-start | bytes 41048 | tf_op jit(solution)/shard_map/ppermute | solution.py:45
  110.9 8.7 %copy-start.8 = (f32[1024]{0:T(1024)S(1)}, f32[1024]{0:T(1024)}, u32[]{:S(2)}) copy-start(f32[1024]{0:T(1024)} %copy-done.7) | copy-start | bytes 12292
  111.0 8.7 %copy-start.11 = (f32[1,1024]{1,0:T(1,128)S(1)}, f32[1,1024]{1,0:T(1,128)}, u32[]{:S(2)}) copy-start(f32[1,1024]{1,0:T(1,128)} %get-tuple-element.90) | copy-start | bytes 12292
  111.0 8.7 %copy-start.12 = (f32[1,1024]{1,0:T(1,128)S(1)}, f32[1,1024]{1,0:T(1,128)}, u32[]{:S(2)}) copy-start(f32[1,1024]{1,0:T(1,128)} %get-tuple-element.91) | copy-start | bytes 12292
  111.0 8.7 %copy-start.13 = (f32[1,1024]{1,0:T(1,128)S(1)}, f32[1,1024]{1,0:T(1,128)}, u32[]{:S(2)}) copy-start(f32[1,1024]{1,0:T(1,128)} %get-tuple-element.92) | copy-start | bytes 12292
  111.0 8.7 %copy-start.14 = (f32[1,1024]{1,0:T(1,128)S(1)}, f32[1,1024]{1,0:T(1,128)}, u32[]{:S(2)}) copy-start(f32[1,1024]{1,0:T(1,128)} %get-tuple-element.83) | copy-start | bytes 12292
  111.0 8.7 %copy-start.15 = (f32[1,1024]{1,0:T(1,128)S(1)}, f32[1,1024]{1,0:T(1,128)}, u32[]{:S(2)}) copy-start(f32[1,1024]{1,0:T(1,128)} %get-tuple-element.84) | copy-start | bytes 12292
  111.0 8.7 %copy-start.16 = (f32[1,1024]{1,0:T(1,128)S(1)}, f32[1,1024]{1,0:T(1,128)}, u32[]{:S(2)}) copy-start(f32[1,1024]{1,0:T(1,128)} %get-tuple-element.85) | copy-start | bytes 12292
  111.0 8.7 %copy-start.17 = (f32[1,1024]{1,0:T(1,128)S(1)}, f32[1,1024]{1,0:T(1,128)}, u32[]{:S(2)}) copy-start(f32[1,1024]{1,0:T(1,128)} %get-tuple-element.86) | copy-start | bytes 12292
  111.0 8.7 %copy-start.18 = (f32[1,1,1,1,1024]{4,3,2,1,0:T(1,128)S(1)}, f32[1,1,1,1,1024]{4,3,2,1,0:T(1,128)}, u32[]{:S(2)}) copy-start(f32[1,1,1,1,1024]{4,3,2,1,0:T(1,128)} %get-tuple-element.93) | copy-start | bytes 12292
  111.0 8.7 %copy-start.19 = (f32[1,1,1,1,1024]{4,3,2,1,0:T(1,128)S(1)}, f32[1,1,1,1,1024]{4,3,2,1,0:T(1,128)}, u32[]{:S(2)}) copy-start(f32[1,1,1,1,1024]{4,3,2,1,0:T(1,128)} %get-tuple-element.94) | copy-start | bytes 12292
  111.1 8.7 %copy-start.10 = (s32[1024]{0:T(1024)S(1)}, s32[1024]{0:T(1024)}, u32[]{:S(2)}) copy-start(s32[1024]{0:T(1024)} %broadcast_select_fusion) | copy-start | bytes 12292
  (13 other events, 78.1 us)
where the time goes:
time: 128 us; the launch traced here: 127 us
  local copies, waits for them, and re-layouts  49.9 us (39%)
  other arithmetic  30.1 us (24%)
  starting transfers between devices  25.4 us (20%)
  waiting for transfers between devices  16.5 us (13%)
  blocking collectives  2.46 us (2%)
  matrix products  1.64 us (1%)
  between operations  1.35 us (1%)
    unnamed x22, other arithmetic  17.6 us
    gather x1, local copies, waits for them, and re-layouts, shards(): post_out = flat_relaxed[link_dirs, cell_idx]  8.59 us
    gather x1, local copies, waits for them, and re-layouts, shards(): current = flat_stream[opp_dir, cell_idx]  8.59 us
    all_to_all x1, starting transfers between devices, shards(): lax.all_to_all(wanted.reshape(owner_count, bucket_cap), ('gx', 'gy'), spl...  8.34 us
    all_to_all x1, waiting for transfers between devices, shards(): lax.all_to_all(outgoing.reshape(6, owner_count, bucket_cap), ('gx', 'gy')...  7.4 us
    all_to_all x1, waiting for transfers between devices, shards(): lax.all_to_all(answer, ('gx', 'gy'), split_axis=1, concat_axis=1, tiled=T...  7.35 us
    slice x4, local copies, waits for them, and re-layouts, padded_2(): lax.slice_in_dim(block, 0, width, axis=dim)  6.77 us
    all_to_all x1, starting transfers between devices, shards(): lax.all_to_all(answer, ('gx', 'gy'), split_axis=1, concat_axis=1, tiled=T...  6.01 us
  transfers between devices with their start and end apart: 9, of which 5 were waited for; matrix products, arithmetic and copies ran while one was open for 35% of the time, Pallas kernels for 0%

commit v1 on v0

v1 whole, which is shorter than its diff:
```python
import functools

import jax
import jax.numpy as jnp
import numpy as np
from jax import lax
from jax.experimental import pallas as pl
from jax.experimental.pallas import tpu as pltpu
from jax.sharding import PartitionSpec as P

VEL = [
    (0, 0, 0), (1, 0, 0), (-1, 0, 0), (0, 1, 0), (0, -1, 0), (0, 0, 1), (0, 0, -1),
    (1, 1, 0), (-1, -1, 0), (1, -1, 0), (-1, 1, 0), (1, 0, 1), (-1, 0, -1), (1, 0, -1),
    (-1, 0, 1), (0, 1, 1), (0, -1, -1), (0, 1, -1), (0, -1, 1),
]
WT = [1.0 / 3.0] + [1.0 / 18.0] * 6 + [1.0 / 36.0] * 12
OPP = [0, 2, 1, 4, 3, 6, 5, 8, 7, 10, 9, 12, 11, 14, 13, 16, 15, 18, 17]
OMEGA = 1.25
GRAV = 0.02
F32 = jnp.float32
BF16 = jnp.bfloat16


def dirs_of(comp, sign):
    return [d for d in range(19) if VEL[d][comp] == sign]


XD = (dirs_of(0, 1), dirs_of(0, -1))
YD = (dirs_of(1, 1), dirs_of(1, -1))
ZD = (dirs_of(2, 1), dirs_of(2, -1))
XZD = tuple([d for d in XD[s] if VEL[d][2] != 0] for s in range(2))


def split3(v):
    hi = v.astype(BF16).astype(F32)
    rest = v - hi
    mid = rest.astype(BF16).astype(F32)
    return hi, mid, rest - mid


def dot(a, b, ca, cb):
    return lax.dot_general(a, b, (((ca,), (cb,)), ((), ())), preferred_element_type=F32)


def stacked(v):
    return jnp.concatenate(split3(v), 0).astype(BF16)


def unstacked(v):
    k = v.shape[0] // 3
    return v[0:k] + v[k : 2 * k] + v[2 * k : 3 * k]


def kernel(
    sizes,
    pop, lcell, ldir, lslot, larm, bb_ref, bpos, bquat, bvel, bspin, imass, iinert,
    nxt, bnext,
    relaxed, sendx, xin, sendz, zin, sende, ein, sendy, yin, yflat, ycols,
    dmap, wmap, motion_own, motion_all, tiles, force_all, half, half_in,
    hs, hr, ms, mr, fs, fr, cs, cr,
):
    ngx, ngy = sizes
    owners = ngx * ngy
    span_x, span_z, span_y = pop.shape[1:]
    cells = span_x * span_z
    links = lcell.shape[-1]
    body_own = bvel.shape[1]
    slots = bb_ref.shape[-1]
    a, b, e = lax.axis_index("gx"), lax.axis_index("gy"), lax.axis_index("gz")
    me = a * ngy + b
    ap, am = lax.rem(a + 1, ngx), lax.rem(a + ngx - 1, ngx)
    bp, bm = lax.rem(b + 1, ngy), lax.rem(b + ngy - 1, ngy)
    oe = 1 - e

    def dev(x, y, z):
        return {"gx": x, "gy": y, "gz": z}

    def peer_of(offset):
        p = lax.rem(me + offset, owners)
        return p, dev(p // ngy, lax.rem(p, ngy), e)

    unroll = owners <= 16

    def loop(lo, hi, body):
        if unroll:
            for i in range(lo, hi):
                body(i)
        else:
            pl.loop(lo, hi)(body)

    barrier = pltpu.get_barrier_semaphore()

    def greet(o):
        pl.semaphore_signal(barrier, inc=1, device_id=peer_of(o)[1], device_id_type=pl.DeviceIdType.MESH)

    loop(1, owners, greet)
    others = [dev(a, b, oe), dev(ap, b, oe), dev(am, b, oe), dev(a, bp, oe), dev(a, bm, oe)]
    for t in others:
        pl.semaphore_signal(barrier, inc=1, device_id=t, device_id_type=pl.DeviceIdType.MESH)

    motion_own[...] = jnp.concatenate(
        [bvel[...], bspin[...], jnp.zeros((2, body_own), F32)], 0
    )
    motion_all[me] = motion_own[...]

    for x in range(span_x):
        for z in range(0, span_z, 8):
            f = [pop[d, x, z : z + 8, :] for d in range(19)]
            rho = f[0]
            for d in range(1, 19):
                rho = rho + f[d]
            inv = 1.0 / rho
            u = []
            for c in range(3):
                pos, neg = dirs_of(c, 1), dirs_of(c, -1)
                tot = f[pos[0]] - f[neg[0]]
                for p, q in zip(pos[1:], neg[1:]):
                    tot = tot + (f[p] - f[q])
                u.append(tot * inv)
            usq = 1.0 - 1.5 * (u[0] * u[0] + u[1] * u[1] + u[2] * u[2])
            rows = pl.ds(x * span_z + z, 8)
            keep = 1.0 - OMEGA
            relaxed[0, rows, :] = keep * f[0] + (OMEGA * WT[0]) * rho * usq
            for d in range(1, 19, 2):
                terms = [u[c] if VEL[d][c] > 0 else -u[c] for c in range(3) if VEL[d][c]]
                proj = terms[0] if len(terms) == 1 else terms[0] + terms[1]
                scale = (OMEGA * WT[d]) * rho
                even = scale * (usq + 4.5 * proj * proj)
                odd = scale * (3.0 * proj)
                relaxed[d, rows, :] = keep * f[d] + (even + odd)
                relaxed[d + 1, rows, :] = keep * f[d + 1] + (even - odd)

    for s in range(2):
        xe = (span_x - 1) if s == 0 else 0
        ze = (span_z - 1) if s == 0 else 0
        for j, d in enumerate(XD[s]):
            sendx[s, j] = relaxed[d, xe * span_z : (xe + 1) * span_z, :]
        for j, d in enumerate(ZD[s]):
            for x in range(span_x):
                r = x * span_z + ze
                sendz[s, j, x : x + 1, :] = relaxed[d, r : r + 1, :]
        sende[s] = jnp.zeros(sende.shape[1:], F32)
        for j, d in enumerate(XZD[s]):
            r = xe * span_z + ((span_z - 1) if VEL[d][2] > 0 else 0)
            sende[s, j : j + 1, :] = relaxed[d, r : r + 1, :]
    lane = lax.broadcasted_iota(jnp.int32, (cells, span_y), 1)
    pack = jnp.zeros((cells, span_y), F32)
    for s in range(2):
        ye = (span_y - 1) if s == 0 else 0
        for j, d in enumerate(YD[s]):
            pack = jnp.where(lane == 8 * s + j, relaxed[d, :, ye : ye + 1], pack)
    pack_t = pack.T
    for s in range(2):
        sendy[s] = pack_t[8 * s : 8 * s + 8, :]

    pl.semaphore_wait(barrier, owners - 1 + len(others))

    def motion_copy(o, slot):
        return pltpu.make_async_remote_copy(
            src_ref=motion_own, dst_ref=motion_all.at[slot], send_sem=ms.at[o], recv_sem=mr.at[slot],
            device_id=peer_of(o)[1], device_id_type=pl.DeviceIdType.MESH,
        )

    loop(1, owners, lambda o: motion_copy(o, me).start())

    halo = []

    def rim(src, dst, target):
        k = len(halo)
        c = pltpu.make_async_remote_copy(
            src_ref=src, dst_ref=dst, send_sem=hs.at[k], recv_sem=hr.at[k],
            device_id=target, device_id_type=pl.DeviceIdType.MESH,
        )
        c.start()
        halo.append(c)

    for s in range(2):
        xt, yt = (ap, bp) if s == 0 else (am, bm)
        rim(sendx.at[s], xin.at[s], dev(xt, b, e))
        rim(sende.at[s], ein.at[s], dev(xt, b, oe))
        rim(sendy.at[s], yin.at[s, 0], dev(a, yt, e))
        rim(sendy.at[s], yin.at[s, 1], dev(ap, yt, e))
        rim(sendy.at[s], yin.at[s, 2], dev(am, yt, e))
        rim(sendy.at[s], yin.at[s, 3], dev(a, yt, oe))
    rim(sendz, zin, dev(a, b, oe))

    cell = lcell[0, 0]
    dirs = ldir[0, 0]
    row_of = cell // span_y
    lane_of = cell - row_of * span_y
    dirs_f = dirs.astype(F32)
    iota_c = lax.broadcasted_iota(jnp.int32, (cells, links), 0)
    iota_y = lax.broadcasted_iota(jnp.int32, (span_y, links), 0)
    row_t = jnp.where(iota_c == row_of, 1.0, 0.0).astype(BF16)
    lane_mask = iota_y == lane_of
    dmap[...] = dot(row_t, jnp.where(lane_mask, dirs_f, 0.0).astype(BF16), 1, 1)
    dm = dmap[...]
    post_map = jnp.zeros((cells, span_y), F32)
    for d in range(1, 19):
        post_map = jnp.where(dm == float(d), relaxed[d], post_map)
    picked = None
    for part in split3(post_map):
        t = dot(part.astype(BF16), row_t, 0, 0)
        picked = t if picked is None else picked + t
    post = jnp.sum(jnp.where(lane_mask, picked, 0.0), axis=0, keepdims=True)
    iota_s = lax.broadcasted_iota(jnp.int32, (slots, links), 0)
    slot_t = jnp.where(iota_s == lslot[0, 0], 1.0, 0.0).astype(BF16)

    vel = []
    for c in range(3):
        v = jnp.zeros((1, links), F32)
        for d in range(1, 19):
            if VEL[d][c]:
                v = jnp.where(dirs == d, float(VEL[d][c]), v)
        vel.append(v)
    six_w = jnp.where(dirs > 6, 6.0 * WT[7], 6.0 * WT[1])

    def motion_wait(o):
        p, _ = peer_of(o)
        motion_copy(o, p).wait_recv()

    loop(1, owners, motion_wait)
    bodies = bb_ref[0, 0]
    iota_b = lax.broadcasted_iota(jnp.int32, (body_own, slots), 0)

    def owner_onehot(o):
        return jnp.where(iota_b == bodies - o * body_own, 1.0, 0.0).astype(BF16)

    def gather(o, acc):
        return acc + dot(stacked(motion_all[o]), owner_onehot(o), 1, 0)

    slot_motion = unstacked(
        lax.fori_loop(0, owners, gather, jnp.zeros((24, slots), F32), unroll=unroll)
    )
    m = unstacked(dot(stacked(slot_motion), slot_t, 1, 0))
    mv = [m[i : i + 1, :] for i in range(6)]
    arm = [larm[i, 0, 0] for i in range(3)]
    wall = [
        mv[0] + mv[4] * arm[2] - mv[5] * arm[1],
        mv[1] + mv[5] * arm[0] - mv[3] * arm[2],
        mv[2] + mv[3] * arm[1] - mv[4] * arm[0],
    ]
    drop = six_w * (vel[0] * wall[0] + vel[1] * wall[1] + vel[2] * wall[2])
    bounce = post - drop
    live = jnp.where(dirs > 0, 1.0, 0.0)
    exchanged = (post + bounce) * live
    force = [vel[c] * exchanged for c in range(3)]
    torque = [
        arm[1] * force[2] - arm[2] * force[1],
        arm[2] * force[0] - arm[0] * force[2],
        arm[0] * force[1] - arm[1] * force[0],
    ]
    loads = jnp.concatenate(force + torque + [jnp.zeros((2, links), F32)], 0)
    slot_load = unstacked(dot(stacked(loads), slot_t, 1, 1))
    slot_parts = stacked(slot_load)

    def spread(o):
        tiles[o] = unstacked(dot(slot_parts, owner_onehot(o), 1, 1))

    loop(0, owners, spread)

    def force_copy(o, src, slot):
        return pltpu.make_async_remote_copy(
            src_ref=tiles.at[src], dst_ref=force_all.at[slot], send_sem=fs.at[o], recv_sem=fr.at[slot],
            device_id=peer_of(o)[1], device_id_type=pl.DeviceIdType.MESH,
        )

    loop(1, owners, lambda o: force_copy(o, peer_of(o)[0], me).start())
    force_all[me] = tiles[me]

    wm = None
    for part in split3(drop):
        t = dot(row_t, jnp.where(lane_mask, part, 0.0).astype(BF16), 1, 1)
        wm = t if wm is None else wm + t
    wmap[...] = wm

    for c in halo:
        c.wait_recv()
    lane_c = lax.broadcasted_iota(jnp.int32, (8, cells), 1)
    z_c = lane_c - (lane_c // span_z) * span_z
    sub_c = lax.broadcasted_iota(jnp.int32, (8, cells), 0)
    both = []
    for s in range(2):
        t0, t1, t2, t3 = (yin[s, k] for k in range(4))
        out = t0
        for j, d in enumerate(YD[s]):
            cx, _, cz = VEL[d]
            if cx == 1:
                v = jnp.where(lane_c < span_z, pltpu.roll(t1, span_z, 1), pltpu.roll(t0, span_z, 1))
            elif cx == -1:
                v = jnp.where(
                    lane_c >= cells - span_z,
                    pltpu.roll(t2, cells - span_z, 1),
                    pltpu.roll(t0, cells - span_z, 1),
                )
            elif cz == 1:
                v = jnp.where(z_c == 0, pltpu.roll(t3, cells - span_z + 1, 1), pltpu.roll(t0, 1, 1))
            elif cz == -1:
                v = jnp.where(
                    z_c == span_z - 1, pltpu.roll(t3, span_z - 1, 1), pltpu.roll(t0, cells - 1, 1)
                )
            else:
                continue
            out = jnp.where(sub_c == j, v, out)
        both.append(out)
    both.append(jnp.zeros((span_y - 16, cells), F32))
    ycols[...] = jnp.concatenate(both, 0).T

    iz = lax.broadcasted_iota(jnp.int32, (span_z, span_y), 0)
    iy = lax.broadcasted_iota(jnp.int32, (span_z, span_y), 1)
    for x in range(span_x):
        rows = slice(x * span_z, (x + 1) * span_z)
        dm_x = dmap[rows, :]
        wm_x = wmap[rows, :]
        for i in range(19):
            cx, cy, cz = VEL[i]
            sx = x - cx
            inside = 0 <= sx < span_x
            if inside:
                v = relaxed[i, sx * span_z : (sx + 1) * span_z, :]
            else:
                s = 0 if cx > 0 else 1
                v = xin[s, XD[s].index(i)]
            if cz:
                s = 0 if cz > 0 else 1
                if inside:
                    edge = zin[s, ZD[s].index(i), sx : sx + 1, :]
                else:
                    sxx = 0 if cx > 0 else 1
                    j = XZD[sxx].index(i)
                    edge = ein[sxx, j : j + 1, :]
                v = pltpu.roll(v, 1 if cz > 0 else span_z - 1, 0)
                v = jnp.where(iz == (0 if cz > 0 else span_z - 1), edge, v)
            if cy:
                s = 0 if cy > 0 else 1
                j = 8 * s + YD[s].index(i)
                v = pltpu.roll(v, 1 if cy > 0 else span_y - 1, 1)
                v = jnp.where(iy == (0 if cy > 0 else span_y - 1), ycols[rows, j : j + 1], v)
            if i:
                d = OPP[i]
                v = jnp.where(dm_x == float(d), relaxed[d, rows, :] - wm_x, v)
            nxt[i, x] = v

    def force_wait(o):
        p, _ = peer_of(o)
        force_copy(o, p, p).wait_recv()

    loop(1, owners, force_wait)
    half[...] = lax.fori_loop(
        0, owners, lambda o, acc: acc + force_all[o], jnp.zeros(half.shape, F32), unroll=unroll
    )
    swap = pltpu.make_async_remote_copy(
        src_ref=half, dst_ref=half_in, send_sem=cs, recv_sem=cr,
        device_id=dev(a, b, oe), device_id_type=pl.DeviceIdType.MESH,
    )
    swap.start()

    def sent(o):
        motion_copy(o, me).wait_send()
        force_copy(o, peer_of(o)[0], me).wait_send()

    loop(1, owners, sent)
    for c in halo:
        c.wait_send()
    swap.wait()
    load = half[...] + half_in[...]
    f = [load[i : i + 1, :] for i in range(6)]
    pos = [bpos[i : i + 1, :] for i in range(3)]
    qw, qx, qy, qz = (bquat[i : i + 1, :] for i in range(4))
    velo = [bvel[i : i + 1, :] + imass[...] * f[i] for i in range(3)]
    velo[2] = velo[2] - GRAV
    rot = [
        [1.0 - 2.0 * (qy * qy + qz * qz), 2.0 * (qx * qy - qw * qz), 2.0 * (qx * qz + qw * qy)],
        [2.0 * (qx * qy + qw * qz), 1.0 - 2.0 * (qx * qx + qz * qz), 2.0 * (qy * qz - qw * qx)],
        [2.0 * (qx * qz - qw * qy), 2.0 * (qy * qz + qw * qx), 1.0 - 2.0 * (qx * qx + qy * qy)],
    ]
    tq = f[3:6]
    acc = [
        iinert[c : c + 1, :] * (rot[0][c] * tq[0] + rot[1][c] * tq[1] + rot[2][c] * tq[2])
        for c in range(3)
    ]
    spin = [
        bspin[r : r + 1, :] + (rot[r][0] * acc[0] + rot[r][1] * acc[1] + rot[r][2] * acc[2])
        for r in range(3)
    ]
    sx, sy, sz = spin
    dq = [
        -(sx * qx + sy * qy + sz * qz),
        sx * qw + sy * qz - sz * qy,
        sy * qw + sz * qx - sx * qz,
        sz * qw + sx * qy - sy * qx,
    ]
    scale = lax.rsqrt(1.0 + 0.25 * (sx * sx + sy * sy + sz * sz))
    quat = [(q + 0.5 * k) * scale for q, k in zip((qw, qx, qy, qz), dq)]
    result = [pos[i] + velo[i] for i in range(3)] + quat + velo + spin
    for i, v in enumerate(result):
        bnext[i : i + 1, :] = v


def shards(sizes, *args):
    pop = args[0]
    span_x, span_z, span_y = pop.shape[1:]
    cells = span_x * span_z
    body_own = args[6].shape[1]
    owners = sizes[0] * sizes[1]
    args = list(args)
    args[10] = args[10].reshape(1, -1)
    vm = pl.BlockSpec(memory_space=pltpu.VMEM)
    dma = pltpu.SemaphoreType.DMA
    V = lambda *s: pltpu.VMEM(s, F32)
    return pl.pallas_call(
        functools.partial(kernel, sizes),
        out_shape=(
            jax.ShapeDtypeStruct(pop.shape, F32),
            jax.ShapeDtypeStruct((13, body_own), F32),
        ),
        in_specs=[vm] * len(args),
        out_specs=(vm, vm),
        scratch_shapes=[
            V(19, cells, span_y),
            V(2, 5, span_z, span_y), V(2, 5, span_z, span_y),
            V(2, 5, span_x, span_y), V(2, 5, span_x, span_y),
            V(2, 8, span_y), V(2, 8, span_y),
            V(2, 8, cells), V(2, 4, 8, cells),
            V(16, cells), V(cells, span_y),
            V(cells, span_y), V(cells, span_y),
            V(8, body_own), V(owners, 8, body_own),
            V(owners, 8, body_own), V(owners, 8, body_own),
            V(8, body_own), V(8, body_own),
            dma((13,)), dma((13,)),
            dma((owners,)), dma((owners,)),
            dma((owners,)), dma((owners,)),
            dma, dma,
        ],
        compiler_params=pltpu.CompilerParams(
            collective_id=0, has_side_effects=True, vmem_limit_bytes=48 * 1024 * 1024
        ),
        name="lattice_step",
    )(*args)


def solution(mesh):
    sizes = (mesh.shape["gx"], mesh.shape["gy"])
    link = P("gx", "gz", "gy", None)
    body = P(None, ("gx", "gy"))
    return jax.shard_map(
        functools.partial(shards, sizes),
        mesh=mesh,
        in_specs=(
            P(None, "gx", "gz", "gy"), link, link, link, P(None, "gx", "gz", "gy", None), link,
            body, body, body, body, P(("gx", "gy")), body,
        ),
        out_specs=(P(None, "gx", "gz", "gy"), body),
        check_vma=False,
    )
```

time: 128 us -> 30.8 us (0.24)
  local copies, waits for them, and re-layouts: 49.9 us -> 10.4 us
  other arithmetic: 30.1 us -> 0 us
  starting transfers between devices: 25.4 us -> 0 us
  Pallas kernels: 0 us -> 19.3 us
  waiting for transfers between devices: 16.5 us -> 0 us
  blocking collectives: 2.46 us -> 0 us
  matrix products: 1.64 us -> 0 us
    pallas_call x0 -> x1, Pallas kernels: none -> 19.3 us  [shards(): pl.pallas_call(functools.partial(kernel, sizes), out_shape=(jax.ShapeDtyp...]
    gather x5 -> x0, local copies, waits for them, and re-layouts: 18.8 us -> none  [the longest x1 8.59 us: shards(): post_out = flat_relaxed[link_dirs, cell_idx]]
    all_to_all x3 -> x0, starting transfers between devices: 17.8 us -> none  [the longest x1 8.34 us: shards(): lax.all_to_all(wanted.reshape(owner_count, bucket_cap), ('gx', 'gy'), spl...]
    unnamed x22 -> x0, other arithmetic: 17.6 us -> none
    all_to_all x3 -> x0, waiting for transfers between devices: 14.8 us -> none  [the longest x1 7.4 us: shards(): lax.all_to_all(outgoing.reshape(6, owner_count, bucket_cap), ('gx', 'gy')...]
    slice x8 -> x0, local copies, waits for them, and re-layouts: 10.5 us -> none  [the longest x4 6.77 us: padded_2(): lax.slice_in_dim(block, 0, width, axis=dim)]
    another operation x3 -> x0, local copies, waits for them, and re-layouts: 8.7 us -> none  [the longest x1 4.34 us: collide(): return jnp.stack(relaxed)]
    unnamed x73 -> x26, local copies, waits for them, and re-layouts: 1.89 us -> 10.4 us
  transfers between devices with their start and end apart: 9 -> 0, of which waited for: 5 -> 0; matrix products, arithmetic and copies ran while one was open for 35% -> 0% of each run, Pallas kernels for 0% -> 0%
where the time goes in v1:
time: 30.8 us; the launch traced here: 30.4 us
  Pallas kernels  19.3 us (63%)
  local copies, waits for them, and re-layouts  10.4 us (34%)
  between operations  0.66 us (2%)
    pallas_call x1, Pallas kernels, shards(): pl.pallas_call(functools.partial(kernel, sizes), out_shape=(jax.ShapeDtyp...  19.3 us
    unnamed x26, local copies, waits for them, and re-layouts  10.4 us

profile of v1, /device:TPU:0, one launch (start us, length us, event | category | flops | bytes accessed | tf_op | source)
XLA Modules:
  0.0 30.4 jit_solution(8628872948522889030)
XLA Ops:
  0.6 0.0 copy-start
  0.6 1.3 %copy-done = f32[19,8,16,128]{3,2,1,0:T(8,128)S(1)} copy-done((f32[19,8,16,128]{3,2,1,0:T(8,128)S(1)}, f32[19,8,16,128]{3,2,1,0:T(8,128)}, u32[]{:S(2)}) %copy-start) | copy-done | bytes 1245208
  1.9 0.0 copy-start.1
  1.9 0.7 %copy-done.1 = f32[3,1,1,1,1024]{4,3,2,1,0:T(1,128)S(1)} copy-done((f32[3,1,1,1,1024]{4,3,2,1,0:T(1,128)S(1)}, f32[3,1,1,1,1024]{4,3,2,1,0:T(1,128)}, u32[]{:S(2)}) %copy-start.1) | copy-done | bytes 12312
  2.6 0.0 copy-start.2
  2.6 0.7 %copy-done.2 = s32[1,1,1,1024]{3,2,1,0:T(1,128)S(1)} copy-done((s32[1,1,1,1024]{3,2,1,0:T(1,128)S(1)}, s32[1,1,1,1024]{3,2,1,0:T(1,128)}, u32[]{:S(2)}) %copy-start.2) | copy-done | bytes 4120
  3.3 0.0 copy-start.3
  3.3 0.7 %copy-done.3 = s32[1,1,1,1024]{3,2,1,0:T(1,128)S(1)} copy-done((s32[1,1,1,1024]{3,2,1,0:T(1,128)S(1)}, s32[1,1,1,1024]{3,2,1,0:T(1,128)}, u32[]{:S(2)}) %copy-start.3) | copy-done | bytes 4120
  4.0 0.0 copy-start.4
  4.0 0.7 %copy-done.4 = s32[1,1,1,1024]{3,2,1,0:T(1,128)S(1)} copy-done((s32[1,1,1,1024]{3,2,1,0:T(1,128)S(1)}, s32[1,1,1,1024]{3,2,1,0:T(1,128)}, u32[]{:S(2)}) %copy-start.4) | copy-done | bytes 4120
  4.7 0.0 copy-start.5
  4.7 0.7 %copy-done.5 = f32[3,128]{1,0:T(4,128)S(1)} copy-done((f32[3,128]{1,0:T(4,128)S(1)}, f32[3,128]{1,0:T(4,128)}, u32[]{:S(2)}) %copy-start.5) | copy-done | bytes 1560
  5.4 0.0 copy-start.6
  5.4 0.7 %copy-done.6 = f32[4,128]{1,0:T(4,128)S(1)} copy-done((f32[4,128]{1,0:T(4,128)S(1)}, f32[4,128]{1,0:T(4,128)}, u32[]{:S(2)}) %copy-start.6) | copy-done | bytes 2072
  6.1 0.0 copy-start.7
  6.1 0.7 %copy-done.7 = f32[3,128]{1,0:T(4,128)S(1)} copy-done((f32[3,128]{1,0:T(4,128)S(1)}, f32[3,128]{1,0:T(4,128)}, u32[]{:S(2)}) %copy-start.7) | copy-done | bytes 1560
  6.7 0.0 copy-start.8
  6.7 0.7 %copy-done.8 = f32[3,128]{1,0:T(4,128)S(1)} copy-done((f32[3,128]{1,0:T(4,128)S(1)}, f32[3,128]{1,0:T(4,128)}, u32[]{:S(2)}) %copy-start.8) | copy-done | bytes 1560
  7.4 0.0 copy-start.9
  7.4 0.7 %copy-done.9 = f32[3,128]{1,0:T(4,128)S(1)} copy-done((f32[3,128]{1,0:T(4,128)S(1)}, f32[3,128]{1,0:T(4,128)}, u32[]{:S(2)}) %copy-start.9) | copy-done | bytes 1560
  8.1 0.0 copy-start.10
  8.1 0.7 %copy-done.10 = s32[1,1,1,128]{3,2,1,0:T(1,128)S(1)} copy-done((s32[1,1,1,128]{3,2,1,0:T(1,128)S(1)}, s32[1,1,1,128]{3,2,1,0:T(1,128)}, u32[]{:S(2)}) %copy-start.10) | copy-done | bytes 536
  8.8 0.0 copy-start.11
  8.8 0.7 %copy-done.11 = f32[128]{0:T(128)S(1)} copy-done((f32[128]{0:T(128)S(1)}, f32[128]{0:T(128)}, u32[]{:S(2)}) %copy-start.11) | copy-done | bytes 536
  9.4 19.3 %lattice_step.1 = (f32[19,8,16,128]{3,2,1,0:T(8,128)S(1)}, f32[13,128]{1,0:T(8,128)S(1)}) custom-call(f32[19,8,16,128]{3,2,1,0:T(8,128)S(1)} %copy-done, s32[1,1,1,1024]{3,2,1,0:T(1,128)S(1)} %copy-done.2, s32[1,1,1,1024]{3,2,1,0:T(1,128)S(1)} %copy-done.3, s32[1,1,1,1024]{3,2,1,0:T(1,128)S(1)} %copy-done.4, f32[3,1,1,1,1024]{4,3,2,1,0:T(1,128)S(1)} %copy-done.1, ...), custom_call_target="tpu_custom_call" | custom-call | tf_op jit(solution)/shard_map/lattice_step/pallas_call | solution.py:411
  28.7 1.0 %copy.16 = f32[19,8,16,128]{3,2,1,0:T(8,128)} copy(f32[19,8,16,128]{3,2,1,0:T(8,128)S(1)} %get-tuple-element.4) | data formatting | bytes 2490368
  29.8 0.6 %copy.17 = f32[13,128]{1,0:T(8,128)} copy(f32[13,128]{1,0:T(8,128)S(1)} %get-tuple-element.5) | data formatting | bytes 13312
Async XLA Ops:
  0.6 1.3 %copy-start = (f32[19,8,16,128]{3,2,1,0:T(8,128)S(1)}, f32[19,8,16,128]{3,2,1,0:T(8,128)}, u32[]{:S(2)}) copy-start(f32[19,8,16,128]{3,2,1,0:T(8,128)} %pop.1) | copy-start | bytes 3735556
  1.9 0.7 %copy-start.1 = (f32[3,1,1,1,1024]{4,3,2,1,0:T(1,128)S(1)}, f32[3,1,1,1,1024]{4,3,2,1,0:T(1,128)}, u32[]{:S(2)}) copy-start(f32[3,1,1,1,1024]{4,3,2,1,0:T(1,128)} %larm.1) | copy-start | bytes 36868
  2.6 0.7 %copy-start.2 = (s32[1,1,1,1024]{3,2,1,0:T(1,128)S(1)}, s32[1,1,1,1024]{3,2,1,0:T(1,128)}, u32[]{:S(2)}) copy-start(s32[1,1,1,1024]{3,2,1,0:T(1,128)} %lcell.1) | copy-start | bytes 12292
  3.3 0.7 %copy-start.3 = (s32[1,1,1,1024]{3,2,1,0:T(1,128)S(1)}, s32[1,1,1,1024]{3,2,1,0:T(1,128)}, u32[]{:S(2)}) copy-start(s32[1,1,1,1024]{3,2,1,0:T(1,128)} %ldir.1) | copy-start | bytes 12292
  4.0 0.7 %copy-start.4 = (s32[1,1,1,1024]{3,2,1,0:T(1,128)S(1)}, s32[1,1,1,1024]{3,2,1,0:T(1,128)}, u32[]{:S(2)}) copy-start(s32[1,1,1,1024]{3,2,1,0:T(1,128)} %lslot.1) | copy-start | bytes 12292
  4.7 0.7 %copy-start.5 = (f32[3,128]{1,0:T(4,128)S(1)}, f32[3,128]{1,0:T(4,128)}, u32[]{:S(2)}) copy-start(f32[3,128]{1,0:T(4,128)} %bpos.1) | copy-start | bytes 4612
  5.4 0.7 %copy-start.6 = (f32[4,128]{1,0:T(4,128)S(1)}, f32[4,128]{1,0:T(4,128)}, u32[]{:S(2)}) copy-start(f32[4,128]{1,0:T(4,128)} %bquat.1) | copy-start | bytes 6148
  6.1 0.7 %copy-start.7 = (f32[3,128]{1,0:T(4,128)S(1)}, f32[3,128]{1,0:T(4,128)}, u32[]{:S(2)}) copy-start(f32[3,128]{1,0:T(4,128)} %bvel.1) | copy-start | bytes 4612
  6.7 0.7 %copy-start.8 = (f32[3,128]{1,0:T(4,128)S(1)}, f32[3,128]{1,0:T(4,128)}, u32[]{:S(2)}) copy-start(f32[3,128]{1,0:T(4,128)} %bspin.1) | copy-start | bytes 4612
  7.4 0.7 %copy-start.9 = (f32[3,128]{1,0:T(4,128)S(1)}, f32[3,128]{1,0:T(4,128)}, u32[]{:S(2)}) copy-start(f32[3,128]{1,0:T(4,128)} %iinert.1) | copy-start | bytes 4612
  8.1 0.7 %copy-start.10 = (s32[1,1,1,128]{3,2,1,0:T(1,128)S(1)}, s32[1,1,1,128]{3,2,1,0:T(1,128)}, u32[]{:S(2)}) copy-start(s32[1,1,1,128]{3,2,1,0:T(1,128)} %bb_ref.1) | copy-start | bytes 1540
  8.8 0.7 %copy-start.11 = (f32[128]{0:T(128)S(1)}, f32[128]{0:T(128)}, u32[]{:S(2)}) copy-start(f32[128]{0:T(128)} %param.22) | copy-start | bytes 1540

commit v2 on v1

--- a/solution.py
+++ b/solution.py
@@ -16,6 +16,9 @@
 WT = [1.0 / 3.0] + [1.0 / 18.0] * 6 + [1.0 / 36.0] * 12
 OPP = [0, 2, 1, 4, 3, 6, 5, 8, 7, 10, 9, 12, 11, 14, 13, 16, 15, 18, 17]
 OMEGA = 1.25
+POP_CHUNKS = 2
+K1_VMEM = 48 * 1024 * 1024
+K2_VMEM = 1024 * 1024
 GRAV = 0.02
 F32 = jnp.float32
 BF16 = jnp.bfloat16
@@ -53,11 +56,20 @@
 
 def kernel(
     sizes,
+    pop_h, *rest,
+):
+    small_h, (nxt, bnext, pop), rest = rest[:11], rest[11:14], rest[14:]
+    small, rest = rest[:11], rest[11:]
+    step(sizes, pop_h, small_h, pop, *small, nxt, bnext, *rest)
+
+
+def step(
+    sizes, pop_h, small_h,
     pop, lcell, ldir, lslot, larm, bb_ref, bpos, bquat, bvel, bspin, imass, iinert,
     nxt, bnext,
     relaxed, sendx, xin, sendz, zin, sende, ein, sendy, yin, yflat, ycols,
     dmap, wmap, motion_own, motion_all, tiles, force_all, half, half_in,
-    hs, hr, ms, mr, fs, fr, cs, cr,
+    hs, hr, ms, mr, fs, fr, cs, cr, ps, ss,
 ):
     ngx, ngy = sizes
     owners = ngx * ngy
@@ -88,6 +100,24 @@
         else:
             pl.loop(lo, hi)(body)
 
+    small = (lcell, ldir, lslot, larm, bb_ref, bpos, bquat, bvel, bspin, imass, iinert)
+    small_in = [
+        pltpu.make_async_copy(src, dst, ss.at[k]) for k, (src, dst) in enumerate(zip(small_h, small))
+    ]
+    chunk = span_x // POP_CHUNKS
+    pop_in = [
+        pltpu.make_async_copy(
+            pop_h.at[:, pl.ds(k * chunk, chunk)], pop.at[:, pl.ds(k * chunk, chunk)], ps.at[k]
+        )
+        for k in range(POP_CHUNKS)
+    ]
+    for k in (7, 8):
+        small_in[k].start()
+    for c in pop_in:
+        c.start()
+    for k in (0, 1, 2, 3, 4, 5, 6, 9, 10):
+        small_in[k].start()
+
     barrier = pltpu.get_barrier_semaphore()
 
     def greet(o):
@@ -98,12 +128,16 @@
     for t in others:
         pl.semaphore_signal(barrier, inc=1, device_id=t, device_id_type=pl.DeviceIdType.MESH)
 
+    small_in[7].wait()
+    small_in[8].wait()
     motion_own[...] = jnp.concatenate(
         [bvel[...], bspin[...], jnp.zeros((2, body_own), F32)], 0
     )
     motion_all[me] = motion_own[...]
 
     for x in range(span_x):
+        if x % chunk == 0:
+            pop_in[x // chunk].wait()
         for z in range(0, span_z, 8):
             f = [pop[d, x, z : z + 8, :] for d in range(19)]
             rho = f[0]
@@ -183,6 +217,9 @@
         rim(sendy.at[s], yin.at[s, 2], dev(am, yt, e))
         rim(sendy.at[s], yin.at[s, 3], dev(a, yt, oe))
     rim(sendz, zin, dev(a, b, oe))
+
+    for k in (0, 1, 2, 3, 4, 5, 6, 9, 10):
+        small_in[k].wait()
 
     cell = lcell[0, 0]
     dirs = ldir[0, 0]
@@ -397,6 +434,14 @@
         bnext[i : i + 1, :] = v
 
 
+def write_out(a, b, a_out, b_out, sems):
+    copies = [pltpu.make_async_copy(a, a_out, sems.at[0]), pltpu.make_async_copy(b, b_out, sems.at[1])]
+    for c in copies:
+        c.start()
+    for c in copies:
+        c.wait()
+
+
 def shards(sizes, *args):
     pop = args[0]
     span_x, span_z, span_y = pop.shape[1:]
@@ -408,15 +453,18 @@
     vm = pl.BlockSpec(memory_space=pltpu.VMEM)
     dma = pltpu.SemaphoreType.DMA
     V = lambda *s: pltpu.VMEM(s, F32)
-    return pl.pallas_call(
+    args = [pltpu.with_memory_space_constraint(v, pltpu.MemorySpace.HBM) for v in args]
+    hbm = pl.BlockSpec(memory_space=pltpu.MemorySpace.HBM)
+    outs = pl.pallas_call(
         functools.partial(kernel, sizes),
         out_shape=(
             jax.ShapeDtypeStruct(pop.shape, F32),
             jax.ShapeDtypeStruct((13, body_own), F32),
         ),
-        in_specs=[vm] * len(args),
+        in_specs=[hbm] * len(args),
         out_specs=(vm, vm),
         scratch_shapes=[
+            *[pltpu.VMEM(v.shape, v.dtype) for v in args],
             V(19, cells, span_y),
             V(2, 5, span_z, span_y), V(2, 5, span_z, span_y),
             V(2, 5, span_x, span_y), V(2, 5, span_x, span_y),
@@ -431,12 +479,22 @@
             dma((owners,)), dma((owners,)),
             dma((owners,)), dma((owners,)),
             dma, dma,
+            dma((POP_CHUNKS,)), dma((11,)),
         ],
         compiler_params=pltpu.CompilerParams(
-            collective_id=0, has_side_effects=True, vmem_limit_bytes=48 * 1024 * 1024
+            collective_id=0, has_side_effects=True, vmem_limit_bytes=K1_VMEM
         ),
         name="lattice_step",
     )(*args)
+    return pl.pallas_call(
+        write_out,
+        out_shape=tuple(jax.ShapeDtypeStruct(v.shape, F32) for v in outs),
+        in_specs=[vm, vm],
+        out_specs=(hbm, hbm),
+        scratch_shapes=[dma((2,))],
+        compiler_params=pltpu.CompilerParams(vmem_limit_bytes=K2_VMEM),
+        name="write_out",
+    )(*outs)
 
 
 def solution(mesh):

time: 30.8 us -> 21.4 us (0.69)
  local copies, waits for them, and re-layouts: 10.4 us -> 0 us
  Pallas kernels: 19.3 us -> 20.5 us
    unnamed x26 -> x0, local copies, waits for them, and re-layouts: 10.4 us -> none
    pallas_call x0 -> x1, Pallas kernels: none -> 1.06 us  [shards(): pl.pallas_call(write_out, out_shape=tuple((jax.ShapeDtypeStruct(v.shape,...]
where the time goes in v2:
time: 21.4 us; the launch traced here: 21.2 us
  Pallas kernels  20.5 us (96%)
  between operations  0.64 us (3%)
    pallas_call x1, Pallas kernels, shards(): pl.pallas_call(functools.partial(kernel, sizes), out_shape=(jax.ShapeDtyp...  19.5 us
    pallas_call x1, Pallas kernels, shards(): pl.pallas_call(write_out, out_shape=tuple((jax.ShapeDtypeStruct(v.shape,...  1.06 us

profile of v2, /device:TPU:0, one launch (start us, length us, event | category | flops | bytes accessed | tf_op | source)
XLA Modules:
  0.0 21.2 jit_solution(15577707202083543986)
XLA Ops:
  0.6 19.5 %lattice_step.1 = (f32[19,8,16,128]{3,2,1,0:T(8,128)S(1)}, f32[13,128]{1,0:T(8,128)S(1)}) custom-call(f32[19,8,16,128]{3,2,1,0:T(8,128)} %pop_h.1, s32[1,1,1,1024]{3,2,1,0:T(1,128)} %rest_0_.1, s32[1,1,1,1024]{3,2,1,0:T(1,128)} %rest_1_.1, s32[1,1,1,1024]{3,2,1,0:T(1,128)} %rest_2_.1, f32[3,1,1,1,1024]{4,3,2,1,0:T(1,128)} %rest_3_.1, ...), custom_call_target="tpu_custom_call" | custom-call | tf_op jit(solution)/shard_map/lattice_step/pallas_call | solution.py:458
  20.1 1.1 %write_out.1 = (f32[19,8,16,128]{3,2,1,0:T(8,128)}, f32[13,128]{1,0:T(8,128)}) custom-call(f32[19,8,16,128]{3,2,1,0:T(8,128)S(1)} %get-tuple-element.4.a, f32[13,128]{1,0:T(8,128)S(1)} %get-tuple-element.5.b), custom_call_target="tpu_custom_call" | custom-call | tf_op jit(solution)/shard_map/write_out/pallas_call | solution.py:489

commit v3 on v2

--- a/solution.py
+++ b/solution.py
@@ -68,10 +68,11 @@
     pop, lcell, ldir, lslot, larm, bb_ref, bpos, bquat, bvel, bspin, imass, iinert,
     nxt, bnext,
     relaxed, sendx, xin, sendz, zin, sende, ein, sendy, yin, yflat, ycols,
-    dmap, wmap, motion_own, motion_all, tiles, force_all, half, half_in,
+    dmap, wmap, motion_own, motion_all, tiles, plane_in, plane_sum, line_in,
     hs, hr, ms, mr, fs, fr, cs, cr, ps, ss,
 ):
-    ngx, ngy = sizes
+    ngx, ngy, ngz = sizes
+    hb = ngy // ngz
     owners = ngx * ngy
     span_x, span_z, span_y = pop.shape[1:]
     cells = span_x * span_z
@@ -87,9 +88,16 @@
     def dev(x, y, z):
         return {"gx": x, "gy": y, "gz": z}
 
-    def peer_of(offset):
-        p = lax.rem(me + offset, owners)
-        return p, dev(p // ngy, lax.rem(p, ngy), e)
+    def step_of(index, count, k):
+        if count & (count - 1) == 0:
+            return jnp.bitwise_xor(index, k)
+        return lax.rem(index + k, count)
+
+    plane = [(k, z) for k in range(ngx) for z in range(ngz) if k or z]
+    line = list(range(1, ngy))
+
+    def plane_dev(k, z):
+        return step_of(a, ngx, k), step_of(e, ngz, z)
 
     unroll = owners <= 16
 
@@ -100,6 +108,14 @@
         else:
             pl.loop(lo, hi)(body)
 
+    barrier = pltpu.get_barrier_semaphore()
+    greeted = [dev(a, step_of(b, ngy, k), z) for k in reversed(line) for z in range(ngz)]
+    for k, z in reversed(plane):
+        x, w = plane_dev(k, z)
+        greeted.append(dev(x, b, w))
+    for t in greeted:
+        pl.semaphore_signal(barrier, inc=1, device_id=t, device_id_type=pl.DeviceIdType.MESH)
+
     small = (lcell, ldir, lslot, larm, bb_ref, bpos, bquat, bvel, bspin, imass, iinert)
     small_in = [
         pltpu.make_async_copy(src, dst, ss.at[k]) for k, (src, dst) in enumerate(zip(small_h, small))
@@ -117,16 +133,6 @@
         c.start()
     for k in (0, 1, 2, 3, 4, 5, 6, 9, 10):
         small_in[k].start()
-
-    barrier = pltpu.get_barrier_semaphore()
-
-    def greet(o):
-        pl.semaphore_signal(barrier, inc=1, device_id=peer_of(o)[1], device_id_type=pl.DeviceIdType.MESH)
-
-    loop(1, owners, greet)
-    others = [dev(a, b, oe), dev(ap, b, oe), dev(am, b, oe), dev(a, bp, oe), dev(a, bm, oe)]
-    for t in others:
-        pl.semaphore_signal(barrier, inc=1, device_id=t, device_id_type=pl.DeviceIdType.MESH)
 
     small_in[7].wait()
     small_in[8].wait()
@@ -187,15 +193,25 @@
     for s in range(2):
         sendy[s] = pack_t[8 * s : 8 * s + 8, :]
 
-    pl.semaphore_wait(barrier, owners - 1 + len(others))
-
-    def motion_copy(o, slot):
+    pl.semaphore_wait(barrier, len(greeted))
+
+    def motion_line(k, slot):
         return pltpu.make_async_remote_copy(
-            src_ref=motion_own, dst_ref=motion_all.at[slot], send_sem=ms.at[o], recv_sem=mr.at[slot],
-            device_id=peer_of(o)[1], device_id_type=pl.DeviceIdType.MESH,
+            src_ref=motion_own, dst_ref=motion_all.at[slot], send_sem=ms.at[k], recv_sem=mr.at[slot],
+            device_id=dev(a, step_of(b, ngy, k), e), device_id_type=pl.DeviceIdType.MESH,
         )
 
-    loop(1, owners, lambda o: motion_copy(o, me).start())
+    def motion_plane(k, kb, src, slot):
+        return pltpu.make_async_remote_copy(
+            src_ref=src, dst_ref=motion_all.at[slot],
+            send_sem=ms.at[k * ngy + kb], recv_sem=mr.at[slot],
+            device_id=dev(step_of(a, ngx, k), b, e), device_id_type=pl.DeviceIdType.MESH,
+        )
+
+    for k in reversed(line):
+        motion_line(k, me).start()
+    for k in range(1, ngx):
+        motion_plane(k, 0, motion_own, me).start()
 
     halo = []
 
@@ -207,15 +223,15 @@
         )
         c.start()
         halo.append(c)
+        return c
+
+    y_rims = []
 
     for s in range(2):
         xt, yt = (ap, bp) if s == 0 else (am, bm)
         rim(sendx.at[s], xin.at[s], dev(xt, b, e))
         rim(sende.at[s], ein.at[s], dev(xt, b, oe))
-        rim(sendy.at[s], yin.at[s, 0], dev(a, yt, e))
-        rim(sendy.at[s], yin.at[s, 1], dev(ap, yt, e))
-        rim(sendy.at[s], yin.at[s, 2], dev(am, yt, e))
-        rim(sendy.at[s], yin.at[s, 3], dev(a, yt, oe))
+        y_rims.append(rim(sendy.at[s], yin.at[s, 0], dev(a, yt, e)))
     rim(sendz, zin, dev(a, b, oe))
 
     for k in (0, 1, 2, 3, 4, 5, 6, 9, 10):
@@ -243,6 +259,20 @@
     iota_s = lax.broadcasted_iota(jnp.int32, (slots, links), 0)
     slot_t = jnp.where(iota_s == lslot[0, 0], 1.0, 0.0).astype(BF16)
 
+    for kb in line:
+        slot = a * ngy + step_of(b, ngy, kb)
+        motion_line(kb, slot).wait_recv()
+        for k in range(1, ngx):
+            motion_plane(k, kb, motion_all.at[slot], slot).start()
+    first = [c for c in halo if all(c is not r for r in y_rims)]
+    for c in y_rims:
+        c.wait_recv()
+    for s in range(2):
+        rim(yin.at[s, 0], yin.at[s, 1], dev(ap, b, e))
+        rim(yin.at[s, 0], yin.at[s, 2], dev(am, b, e))
+        rim(yin.at[s, 0], yin.at[s, 3], dev(a, b, oe))
+    second = halo[len(first) + len(y_rims) :]
+
     vel = []
     for c in range(3):
         v = jnp.zeros((1, links), F32)
@@ -252,11 +282,10 @@
         vel.append(v)
     six_w = jnp.where(dirs > 6, 6.0 * WT[7], 6.0 * WT[1])
 
-    def motion_wait(o):
-        p, _ = peer_of(o)
-        motion_copy(o, p).wait_recv()
-
-    loop(1, owners, motion_wait)
+    for kb in range(ngy):
+        for k in range(1, ngx):
+            slot = step_of(a, ngx, k) * ngy + step_of(b, ngy, kb)
+            motion_plane(k, kb, motion_own, slot).wait_recv()
     bodies = bb_ref[0, 0]
     iota_b = lax.broadcasted_iota(jnp.int32, (body_own, slots), 0)
 
@@ -296,14 +325,20 @@
 
     loop(0, owners, spread)
 
-    def force_copy(o, src, slot):
+    here = a * ngz + e
+
+    def force_plane(k, z, slot):
+        x, w = plane_dev(k, z)
         return pltpu.make_async_remote_copy(
-            src_ref=tiles.at[src], dst_ref=force_all.at[slot], send_sem=fs.at[o], recv_sem=fr.at[slot],
-            device_id=peer_of(o)[1], device_id_type=pl.DeviceIdType.MESH,
+            src_ref=tiles.at[pl.ds(x * ngy + w * hb, hb)], dst_ref=plane_in.at[slot],
+            send_sem=fs.at[k * ngz + z], recv_sem=fr.at[slot],
+            device_id=dev(x, b, w), device_id_type=pl.DeviceIdType.MESH,
         )
 
-    loop(1, owners, lambda o: force_copy(o, peer_of(o)[0], me).start())
-    force_all[me] = tiles[me]
+    for k, z in reversed(plane):
+        force_plane(k, z, here).start()
+    for k in range(hb):
+        plane_in[here, k] = tiles[a * ngy + e * hb + k]
 
     wm = None
     for part in split3(drop):
@@ -311,7 +346,7 @@
         wm = t if wm is None else wm + t
     wmap[...] = wm
 
-    for c in halo:
+    for c in first + second:
         c.wait_recv()
     lane_c = lax.broadcasted_iota(jnp.int32, (8, cells), 1)
     z_c = lane_c - (lane_c // span_z) * span_z
@@ -345,7 +380,8 @@
 
     iz = lax.broadcasted_iota(jnp.int32, (span_z, span_y), 0)
     iy = lax.broadcasted_iota(jnp.int32, (span_z, span_y), 1)
-    for x in range(span_x):
+
+    def stream(x):
         rows = slice(x * span_z, (x + 1) * span_z)
         dm_x = dmap[rows, :]
         wm_x = wmap[rows, :]
@@ -378,29 +414,66 @@
                 v = jnp.where(dm_x == float(d), relaxed[d, rows, :] - wm_x, v)
             nxt[i, x] = v
 
-    def force_wait(o):
-        p, _ = peer_of(o)
-        force_copy(o, p, p).wait_recv()
-
-    loop(1, owners, force_wait)
-    half[...] = lax.fori_loop(
-        0, owners, lambda o, acc: acc + force_all[o], jnp.zeros(half.shape, F32), unroll=unroll
-    )
-    swap = pltpu.make_async_remote_copy(
-        src_ref=half, dst_ref=half_in, send_sem=cs, recv_sem=cr,
-        device_id=dev(a, b, oe), device_id_type=pl.DeviceIdType.MESH,
-    )
-    swap.start()
-
-    def sent(o):
-        motion_copy(o, me).wait_send()
-        force_copy(o, peer_of(o)[0], me).wait_send()
-
-    loop(1, owners, sent)
+    for x in range(span_x // 2):
+        stream(x)
+
+    for k, z in plane:
+        x, w = plane_dev(k, z)
+        force_plane(k, z, x * ngz + w).wait_recv()
+    total = plane_in[0]
+    for k in range(1, ngx * ngz):
+        total = total + plane_in[k]
+    plane_sum[...] = total
+
+    def force_line(k, z, src_b):
+        return pltpu.make_async_remote_copy(
+            src_ref=plane_sum.at[k], dst_ref=line_in.at[src_b],
+            send_sem=cs.at[k * ngz + z], recv_sem=cr.at[src_b],
+            device_id=dev(a, e * hb + k, z), device_id_type=pl.DeviceIdType.MESH,
+        )
+
+    for k in range(hb):
+        for z in range(ngz):
+            mine = (e * hb + k == b) & (e == z)
+
+            @pl.when(jnp.logical_not(mine))
+            def _():
+                force_line(k, z, b).start()
+
+            @pl.when(mine)
+            def _():
+                line_in[b] = plane_sum[k]
+
+    for x in range(span_x // 2, span_x):
+        stream(x)
+
+    for k in line:
+        motion_line(k, me).wait_send()
+    for kb in range(ngy):
+        for k in range(1, ngx):
+            motion_plane(k, kb, motion_own, me).wait_send()
+    for k, z in plane:
+        force_plane(k, z, here).wait_send()
     for c in halo:
         c.wait_send()
-    swap.wait()
-    load = half[...] + half_in[...]
+    for src in range(ngy):
+        local = (b // hb == e) & (b == src)
+
+        @pl.when(jnp.logical_not(local))
+        def _():
+            force_line(0, 0, src).wait_recv()
+
+    load = line_in[0]
+    for k in range(1, ngy):
+        load = load + line_in[k]
+    for k in range(hb):
+        for z in range(ngz):
+            mine = (e * hb + k == b) & (e == z)
+
+            @pl.when(jnp.logical_not(mine))
+            def _():
+                force_line(k, z, b).wait_send()
+
     f = [load[i : i + 1, :] for i in range(6)]
     pos = [bpos[i : i + 1, :] for i in range(3)]
     qw, qx, qy, qz = (bquat[i : i + 1, :] for i in range(4))
@@ -447,7 +520,8 @@
     span_x, span_z, span_y = pop.shape[1:]
     cells = span_x * span_z
     body_own = args[6].shape[1]
-    owners = sizes[0] * sizes[1]
+    ngx, ngy, ngz = sizes
+    owners = ngx * ngy
     args = list(args)
     args[10] = args[10].reshape(1, -1)
     vm = pl.BlockSpec(memory_space=pltpu.VMEM)
@@ -473,12 +547,12 @@
             V(16, cells), V(cells, span_y),
             V(cells, span_y), V(cells, span_y),
             V(8, body_own), V(owners, 8, body_own),
-            V(owners, 8, body_own), V(owners, 8, body_own),
-            V(8, body_own), V(8, body_own),
+            V(owners, 8, body_own), V(ngx * ngz, ngy // ngz, 8, body_own),
+            V(ngy // ngz, 8, body_own), V(ngy, 8, body_own),
             dma((13,)), dma((13,)),
             dma((owners,)), dma((owners,)),
-            dma((owners,)), dma((owners,)),
-            dma, dma,
+            dma((ngx * ngz,)), dma((ngx * ngz,)),
+            dma((ngy,)), dma((ngy,)),
             dma((POP_CHUNKS,)), dma((11,)),
         ],
         compiler_params=pltpu.CompilerParams(
@@ -498,7 +572,7 @@
 
 
 def solution(mesh):
-    sizes = (mesh.shape["gx"], mesh.shape["gy"])
+    sizes = (mesh.shape["gx"], mesh.shape["gy"], mesh.shape["gz"])
     link = P("gx", "gz", "gy", None)
     body = P(None, ("gx", "gy"))
     return jax.shard_map(

time: 21.4 us -> 22.8 us (1.065)
  Pallas kernels: 20.5 us -> 22 us
    pallas_call x1, Pallas kernels: 19.5 us -> 20.9 us  [shards(): pl.pallas_call(functools.partial(kernel, sizes), out_shape=(jax.ShapeDtyp...]
where the time goes in v3:
time: 22.8 us; the launch traced here: 22.6 us
  Pallas kernels  22 us (96%)
  between operations  0.64 us (3%)
    pallas_call x1, Pallas kernels, shards(): pl.pallas_call(functools.partial(kernel, sizes), out_shape=(jax.ShapeDtyp...  20.9 us
    pallas_call x1, Pallas kernels, shards(): pl.pallas_call(write_out, out_shape=tuple((jax.ShapeDtypeStruct(v.shape,...  1.06 us

profile of v3, /device:TPU:0, one launch (start us, length us, event | category | flops | bytes accessed | tf_op | source)
XLA Modules:
  0.0 22.6 jit_solution(2961224868986561281)
XLA Ops:
  0.6 20.9 %lattice_step.1 = (f32[19,8,16,128]{3,2,1,0:T(8,128)S(1)}, f32[13,128]{1,0:T(8,128)S(1)}) custom-call(f32[19,8,16,128]{3,2,1,0:T(8,128)} %pop_h.1, s32[1,1,1,1024]{3,2,1,0:T(1,128)} %rest_0_.1, s32[1,1,1,1024]{3,2,1,0:T(1,128)} %rest_1_.1, s32[1,1,1,1024]{3,2,1,0:T(1,128)} %rest_2_.1, f32[3,1,1,1,1024]{4,3,2,1,0:T(1,128)} %rest_3_.1, ...), custom_call_target="tpu_custom_call" | custom-call | tf_op jit(solution)/shard_map/lattice_step/pallas_call | solution.py:532
  21.5 1.1 %write_out.1 = (f32[19,8,16,128]{3,2,1,0:T(8,128)}, f32[13,128]{1,0:T(8,128)}) custom-call(f32[19,8,16,128]{3,2,1,0:T(8,128)S(1)} %get-tuple-element.4.a, f32[13,128]{1,0:T(8,128)S(1)} %get-tuple-element.5.b), custom_call_target="tpu_custom_call" | custom-call | tf_op jit(solution)/shard_map/write_out/pallas_call | solution.py:563

commit v4 on v3

--- a/solution.py
+++ b/solution.py
@@ -68,7 +68,7 @@
     pop, lcell, ldir, lslot, larm, bb_ref, bpos, bquat, bvel, bspin, imass, iinert,
     nxt, bnext,
     relaxed, sendx, xin, sendz, zin, sende, ein, sendy, yin, yflat, ycols,
-    dmap, wmap, motion_own, motion_all, tiles, plane_in, plane_sum, line_in,
+    dmap, wmap, motion_own, motion_all, tiles, plane_in, plane_sum, line_in, picks,
     hs, hr, ms, mr, fs, fr, cs, cr, ps, ss,
 ):
     ngx, ngy, ngz = sizes
@@ -88,6 +88,10 @@
     def dev(x, y, z):
         return {"gx": x, "gy": y, "gz": z}
 
+    def peer_of(offset):
+        p = lax.rem(me + offset, owners)
+        return p, dev(p // ngy, lax.rem(p, ngy), e)
+
     def step_of(index, count, k):
         if count & (count - 1) == 0:
             return jnp.bitwise_xor(index, k)
@@ -109,11 +113,14 @@
             pl.loop(lo, hi)(body)
 
     barrier = pltpu.get_barrier_semaphore()
-    greeted = [dev(a, step_of(b, ngy, k), z) for k in reversed(line) for z in range(ngz)]
-    for k, z in reversed(plane):
-        x, w = plane_dev(k, z)
-        greeted.append(dev(x, b, w))
-    for t in greeted:
+
+    def greet(o):
+        pl.semaphore_signal(barrier, inc=1, device_id=peer_of(o)[1], device_id_type=pl.DeviceIdType.MESH)
+
+    loop(1, owners, greet)
+    others = [dev(step_of(a, ngx, k), b, oe) for k in range(ngx)]
+    others += [dev(a, step_of(b, ngy, k), oe) for k in line]
+    for t in others:
         pl.semaphore_signal(barrier, inc=1, device_id=t, device_id_type=pl.DeviceIdType.MESH)
 
     small = (lcell, ldir, lslot, larm, bb_ref, bpos, bquat, bvel, bspin, imass, iinert)
@@ -193,25 +200,15 @@
     for s in range(2):
         sendy[s] = pack_t[8 * s : 8 * s + 8, :]
 
-    pl.semaphore_wait(barrier, len(greeted))
-
-    def motion_line(k, slot):
+    pl.semaphore_wait(barrier, owners - 1 + len(others))
+
+    def motion_copy(o, slot):
         return pltpu.make_async_remote_copy(
-            src_ref=motion_own, dst_ref=motion_all.at[slot], send_sem=ms.at[k], recv_sem=mr.at[slot],
-            device_id=dev(a, step_of(b, ngy, k), e), device_id_type=pl.DeviceIdType.MESH,
+            src_ref=motion_own, dst_ref=motion_all.at[slot], send_sem=ms.at[o], recv_sem=mr.at[slot],
+            device_id=peer_of(o)[1], device_id_type=pl.DeviceIdType.MESH,
         )
 
-    def motion_plane(k, kb, src, slot):
-        return pltpu.make_async_remote_copy(
-            src_ref=src, dst_ref=motion_all.at[slot],
-            send_sem=ms.at[k * ngy + kb], recv_sem=mr.at[slot],
-            device_id=dev(step_of(a, ngx, k), b, e), device_id_type=pl.DeviceIdType.MESH,
-        )
-
-    for k in reversed(line):
-        motion_line(k, me).start()
-    for k in range(1, ngx):
-        motion_plane(k, 0, motion_own, me).start()
+    loop(1, owners, lambda o: motion_copy(o, me).start())
 
     halo = []
 
@@ -223,15 +220,15 @@
         )
         c.start()
         halo.append(c)
-        return c
-
-    y_rims = []
 
     for s in range(2):
         xt, yt = (ap, bp) if s == 0 else (am, bm)
         rim(sendx.at[s], xin.at[s], dev(xt, b, e))
         rim(sende.at[s], ein.at[s], dev(xt, b, oe))
-        y_rims.append(rim(sendy.at[s], yin.at[s, 0], dev(a, yt, e)))
+        rim(sendy.at[s], yin.at[s, 0], dev(a, yt, e))
+        rim(sendy.at[s], yin.at[s, 1], dev(ap, yt, e))
+        rim(sendy.at[s], yin.at[s, 2], dev(am, yt, e))
+        rim(sendy.at[s], yin.at[s, 3], dev(a, yt, oe))
     rim(sendz, zin, dev(a, b, oe))
 
     for k in (0, 1, 2, 3, 4, 5, 6, 9, 10):
@@ -259,20 +256,6 @@
     iota_s = lax.broadcasted_iota(jnp.int32, (slots, links), 0)
     slot_t = jnp.where(iota_s == lslot[0, 0], 1.0, 0.0).astype(BF16)
 
-    for kb in line:
-        slot = a * ngy + step_of(b, ngy, kb)
-        motion_line(kb, slot).wait_recv()
-        for k in range(1, ngx):
-            motion_plane(k, kb, motion_all.at[slot], slot).start()
-    first = [c for c in halo if all(c is not r for r in y_rims)]
-    for c in y_rims:
-        c.wait_recv()
-    for s in range(2):
-        rim(yin.at[s, 0], yin.at[s, 1], dev(ap, b, e))
-        rim(yin.at[s, 0], yin.at[s, 2], dev(am, b, e))
-        rim(yin.at[s, 0], yin.at[s, 3], dev(a, b, oe))
-    second = halo[len(first) + len(y_rims) :]
-
     vel = []
     for c in range(3):
         v = jnp.zeros((1, links), F32)
@@ -282,21 +265,21 @@
         vel.append(v)
     six_w = jnp.where(dirs > 6, 6.0 * WT[7], 6.0 * WT[1])
 
-    for kb in range(ngy):
-        for k in range(1, ngx):
-            slot = step_of(a, ngx, k) * ngy + step_of(b, ngy, kb)
-            motion_plane(k, kb, motion_own, slot).wait_recv()
     bodies = bb_ref[0, 0]
     iota_b = lax.broadcasted_iota(jnp.int32, (body_own, slots), 0)
 
-    def owner_onehot(o):
-        return jnp.where(iota_b == bodies - o * body_own, 1.0, 0.0).astype(BF16)
+    def pick(o):
+        picks[o] = jnp.where(iota_b == bodies - o * body_own, 1.0, 0.0).astype(BF16)
+
+    loop(0, owners, pick)
 
     def gather(o, acc):
-        return acc + dot(stacked(motion_all[o]), owner_onehot(o), 1, 0)
+        p, _ = peer_of(o)
+        motion_copy(o, p).wait_recv()
+        return acc + dot(stacked(motion_all[p]), picks[p], 1, 0)
 
     slot_motion = unstacked(
-        lax.fori_loop(0, owners, gather, jnp.zeros((24, slots), F32), unroll=unroll)
+        lax.fori_loop(1, owners, gather, dot(stacked(motion_all[me]), picks[me], 1, 0), unroll=unroll)
     )
     m = unstacked(dot(stacked(slot_motion), slot_t, 1, 0))
     mv = [m[i : i + 1, :] for i in range(6)]
@@ -321,7 +304,7 @@
     slot_parts = stacked(slot_load)
 
     def spread(o):
-        tiles[o] = unstacked(dot(slot_parts, owner_onehot(o), 1, 1))
+        tiles[o] = unstacked(dot(slot_parts, picks[o], 1, 1))
 
     loop(0, owners, spread)
 
@@ -346,7 +329,7 @@
         wm = t if wm is None else wm + t
     wmap[...] = wm
 
-    for c in first + second:
+    for c in halo:
         c.wait_recv()
     lane_c = lax.broadcasted_iota(jnp.int32, (8, cells), 1)
     z_c = lane_c - (lane_c // span_z) * span_z
@@ -447,11 +430,7 @@
     for x in range(span_x // 2, span_x):
         stream(x)
 
-    for k in line:
-        motion_line(k, me).wait_send()
-    for kb in range(ngy):
-        for k in range(1, ngx):
-            motion_plane(k, kb, motion_own, me).wait_send()
+    loop(1, owners, lambda o: motion_copy(o, me).wait_send())
     for k, z in plane:
         force_plane(k, z, here).wait_send()
     for c in halo:
@@ -549,6 +528,7 @@
             V(8, body_own), V(owners, 8, body_own),
             V(owners, 8, body_own), V(ngx * ngz, ngy // ngz, 8, body_own),
             V(ngy // ngz, 8, body_own), V(ngy, 8, body_own),
+            pltpu.VMEM((owners, body_own, args[5].shape[-1]), BF16),
             dma((13,)), dma((13,)),
             dma((owners,)), dma((owners,)),
             dma((ngx * ngz,)), dma((ngx * ngz,)),

time: 22.8 us -> 24.3 us (1.066)
  Pallas kernels: 22 us -> 23.5 us
    pallas_call x1, Pallas kernels: 20.9 us -> 22.4 us  [shards(): pl.pallas_call(functools.partial(kernel, sizes), out_shape=(jax.ShapeDtyp...]
where the time goes in v4:
time: 24.3 us; the launch traced here: 24.1 us
  Pallas kernels  23.5 us (97%)
  between operations  0.64 us (3%)
    pallas_call x1, Pallas kernels, shards(): pl.pallas_call(functools.partial(kernel, sizes), out_shape=(jax.ShapeDtyp...  22.4 us
    pallas_call x1, Pallas kernels, shards(): pl.pallas_call(write_out, out_shape=tuple((jax.ShapeDtypeStruct(v.shape,...  1.06 us

profile of v4, /device:TPU:0, one launch (start us, length us, event | category | flops | bytes accessed | tf_op | source)
XLA Modules:
  0.0 24.1 jit_solution(1619359746175164944)
XLA Ops:
  0.6 22.4 %lattice_step.1 = (f32[19,8,16,128]{3,2,1,0:T(8,128)S(1)}, f32[13,128]{1,0:T(8,128)S(1)}) custom-call(f32[19,8,16,128]{3,2,1,0:T(8,128)} %pop_h.1, s32[1,1,1,1024]{3,2,1,0:T(1,128)} %rest_0_.1, s32[1,1,1,1024]{3,2,1,0:T(1,128)} %rest_1_.1, s32[1,1,1,1024]{3,2,1,0:T(1,128)} %rest_2_.1, f32[3,1,1,1,1024]{4,3,2,1,0:T(1,128)} %rest_3_.1, ...), custom_call_target="tpu_custom_call" | custom-call | tf_op jit(solution)/shard_map/lattice_step/pallas_call | solution.py:511
  23.1 1.1 %write_out.1 = (f32[19,8,16,128]{3,2,1,0:T(8,128)}, f32[13,128]{1,0:T(8,128)}) custom-call(f32[19,8,16,128]{3,2,1,0:T(8,128)S(1)} %get-tuple-element.4.a, f32[13,128]{1,0:T(8,128)S(1)} %get-tuple-element.5.b), custom_call_target="tpu_custom_call" | custom-call | tf_op jit(solution)/shard_map/write_out/pallas_call | solution.py:543

commit v5 on v4

--- a/solution.py
+++ b/solution.py
@@ -274,12 +274,11 @@
     loop(0, owners, pick)
 
     def gather(o, acc):
-        p, _ = peer_of(o)
-        motion_copy(o, p).wait_recv()
-        return acc + dot(stacked(motion_all[p]), picks[p], 1, 0)
-
+        return acc + dot(stacked(motion_all[o]), picks[o], 1, 0)
+
+    loop(1, owners, lambda o: motion_copy(o, peer_of(o)[0]).wait_recv())
     slot_motion = unstacked(
-        lax.fori_loop(1, owners, gather, dot(stacked(motion_all[me]), picks[me], 1, 0), unroll=unroll)
+        lax.fori_loop(0, owners, gather, jnp.zeros((24, slots), F32), unroll=unroll)
     )
     m = unstacked(dot(stacked(slot_motion), slot_t, 1, 0))
     mv = [m[i : i + 1, :] for i in range(6)]

time: 24.3 us -> 22.7 us (0.934)
  Pallas kernels: 23.5 us -> 21.9 us
    pallas_call x1, Pallas kernels: 22.4 us -> 20.8 us  [shards(): pl.pallas_call(functools.partial(kernel, sizes), out_shape=(jax.ShapeDtyp...]
where the time goes in v5:
time: 22.7 us; the launch traced here: 22.5 us
  Pallas kernels  21.9 us (96%)
  between operations  0.64 us (3%)
    pallas_call x1, Pallas kernels, shards(): pl.pallas_call(functools.partial(kernel, sizes), out_shape=(jax.ShapeDtyp...  20.8 us
    pallas_call x1, Pallas kernels, shards(): pl.pallas_call(write_out, out_shape=tuple((jax.ShapeDtypeStruct(v.shape,...  1.06 us

profile of v5, /device:TPU:0, one launch (start us, length us, event | category | flops | bytes accessed | tf_op | source)
XLA Modules:
  0.0 22.5 jit_solution(9815112176510531018)
XLA Ops:
  0.6 20.8 %lattice_step.1 = (f32[19,8,16,128]{3,2,1,0:T(8,128)S(1)}, f32[13,128]{1,0:T(8,128)S(1)}) custom-call(f32[19,8,16,128]{3,2,1,0:T(8,128)} %pop_h.1, s32[1,1,1,1024]{3,2,1,0:T(1,128)} %rest_0_.1, s32[1,1,1,1024]{3,2,1,0:T(1,128)} %rest_1_.1, s32[1,1,1,1024]{3,2,1,0:T(1,128)} %rest_2_.1, f32[3,1,1,1,1024]{4,3,2,1,0:T(1,128)} %rest_3_.1, ...), custom_call_target="tpu_custom_call" | custom-call | tf_op jit(solution)/shard_map/lattice_step/pallas_call | solution.py:510
  21.5 1.1 %write_out.1 = (f32[19,8,16,128]{3,2,1,0:T(8,128)}, f32[13,128]{1,0:T(8,128)}) custom-call(f32[19,8,16,128]{3,2,1,0:T(8,128)S(1)} %get-tuple-element.4.a, f32[13,128]{1,0:T(8,128)S(1)} %get-tuple-element.5.b), custom_call_target="tpu_custom_call" | custom-call | tf_op jit(solution)/shard_map/write_out/pallas_call | solution.py:542
